TPU v7x, 512 devices: a whole 4x8x8 slice. The times are simulated.
512 devices in a mesh: section: 16 (over y, z_hi), dp: 32 (over z_lo, x, core).
Axes of the slice: x: 4, y: 8, z: 8 (z_hi: 2, z_lo: 4; z = z_hi * 4 + z_lo), core: 2. Of those that a mesh axis runs over, the one named last changes fastest.
Arguments:
- section_input: bfloat16 [6, 768, 3072], P(None, 'dp'), may hold values from -6 to 6
- loss_grad: bfloat16 [6, 768, 3072], P(None, 'dp'), may hold values from -6 to 6
- norm_gain: float32 [16, 3072], P('section'), may hold values from 0.1 to 1.9
- channel_order: int32 [16, 3072], P('section'), may hold values from 0 to 3071, each once within a row
- right_factor: bfloat16 [16, 3072, 768], P('section', 'dp'), may hold values from -0.15625 to 0.15625
- left_factor: bfloat16 [16, 3072, 768], P('section', 'dp'), may hold values from -0.15625 to 0.15625
Outputs:
- section_output: bfloat16 [16, 6, 768, 3072], P('section', None, 'dp')
- left_grad: float32 [16, 768, 768], P('section', 'dp')
Inputs may be any that keep to these rules, and one draw needn't show every extreme that they name: `channel_order`: each layer's row is a permutation of the 3072 channels.
All inputs are finite; a program needn't handle non-finite values.
Results may differ from a plain program's by a relative error of at most 0.03.
Values may be sent and summed in bfloat16 or wider, within the bound.
A program may use at most 64 MiB of HBM per device.

v0:
```python
import jax
import jax.numpy as jnp
from jax import lax
from jax.sharding import PartitionSpec as P

epsilon = 1e-05


def shifted(array, axis, by):
    peers = lax.axis_size(axis)
    pairs = [(i, i + by) for i in range(peers) if 0 <= i + by < peers]
    return lax.ppermute(array, axis, pairs)


def block_apply(values, factor):
    row_count = values.shape[0]
    block_size = factor.shape[1]
    block_count = factor.shape[0] // block_size
    result = jnp.einsum(
        "rnk,nkj->rnj",
        values.reshape(row_count, block_count, block_size),
        factor.reshape(block_count, block_size, block_size),
        preferred_element_type=jnp.float32,
    )
    return result.reshape(row_count, block_count * block_size)


def block_transposed(values, factor):
    row_count = values.shape[0]
    block_size = factor.shape[1]
    block_count = factor.shape[0] // block_size
    result = jnp.einsum(
        "rnj,nkj->rnk",
        values.reshape(row_count, block_count, block_size),
        factor.reshape(block_count, block_size, block_size),
        preferred_element_type=jnp.float32,
    )
    return result.reshape(row_count, block_count * block_size)


def inverse_norm(inputs):
    wide_in = inputs.astype(jnp.float32)
    return (wide_in, lax.rsqrt(jnp.mean(wide_in * wide_in, axis=-1, keepdims=True) + epsilon))


def layer_forward(inputs, gain_row, shuffle, right_full, left_full):
    wide_in, inverse_rms = inverse_norm(inputs)
    normed = (wide_in * inverse_rms * gain_row).astype(jnp.bfloat16)
    mixed = block_apply(normed, right_full).astype(jnp.bfloat16)
    permuted = jnp.take(mixed, shuffle, axis=1)
    output = (wide_in + block_apply(permuted, left_full)).astype(jnp.bfloat16)
    return (output, permuted)


def layer_backward(inputs, upstream, gain_row, inverse, right_full, left_full):
    wide_in, inverse_rms = inverse_norm(inputs)
    through = block_transposed(upstream, left_full).astype(jnp.bfloat16)
    before = jnp.take(through, inverse, axis=1)
    scaled = block_transposed(before, right_full) * gain_row
    cubed = inverse_rms * inverse_rms * inverse_rms
    grad_input = (
        upstream.astype(jnp.float32)
        + inverse_rms * scaled
        - wide_in * cubed * jnp.mean(scaled * wide_in, axis=-1, keepdims=True)
    )
    return grad_input.astype(jnp.bfloat16)


def store_slot(buffer, batch_slot, is_valid, new_value):
    old_value = lax.dynamic_index_in_dim(buffer, batch_slot, 0, keepdims=False)
    return lax.dynamic_update_index_in_dim(
        buffer, jnp.where(is_valid, new_value, old_value), batch_slot, 0
    )


def per_device(section_input, loss_grad, norm_gain, channel_order, right_factor, left_factor):
    sections = lax.axis_size("section")
    section_index = lax.axis_index("section")
    micro_count, row_count, channels = section_input.shape
    block_size = right_factor.shape[2]
    right_full, left_full = (
        lax.all_gather(right_factor[0], "dp", axis=0, tiled=True),
        lax.all_gather(left_factor[0], "dp", axis=0, tiled=True),
    )
    gain_row = norm_gain[0]
    shuffle = channel_order[0]
    inverse = (
        jnp.zeros((channels,), jnp.int32).at[shuffle].set(jnp.arange(channels, dtype=jnp.int32))
    )
    empty_buf = jnp.zeros((micro_count, row_count, channels), jnp.bfloat16)
    empty_head = jnp.zeros((micro_count, row_count, block_size), jnp.bfloat16)
    empty_rows = jnp.zeros((row_count, channels), jnp.bfloat16)
    is_first = section_index == 0
    is_last = section_index == sections - 1

    def run_forward(inputs):
        output, permuted = layer_forward(inputs, gain_row, shuffle, right_full, left_full)
        return (output, permuted[:, :block_size])

    def skip_forward(inputs):
        return (jnp.zeros_like(inputs), jnp.zeros((row_count, block_size), jnp.bfloat16))

    def run_backward(operands):
        return layer_backward(operands[0], operands[1], gain_row, inverse, right_full, left_full)

    def skip_backward(operands):
        return jnp.zeros_like(operands[1])

    def forward_part(forward_state, step_num):
        incoming, saved_in, saved_permuted, outputs = forward_state
        batch_pos = step_num - section_index
        is_valid = (batch_pos >= 0) & (batch_pos < micro_count)
        batch_slot = jnp.clip(batch_pos, 0, micro_count - 1)
        inputs = jnp.where(
            is_first,
            lax.dynamic_index_in_dim(section_input, batch_slot, 0, keepdims=False),
            incoming,
        )
        output, permuted_head = lax.cond(is_valid, run_forward, skip_forward, inputs)
        saved_in = store_slot(saved_in, batch_slot, is_valid, inputs)
        saved_permuted = store_slot(saved_permuted, batch_slot, is_valid, permuted_head)
        outputs = store_slot(outputs, batch_slot, is_valid, output)
        passed = shifted(output, "section", 1)
        return (passed, saved_in, saved_permuted, outputs)

    def backward_part(backward_state, saved_in, step_num, lag_steps):
        incoming, saved_upstream = backward_state
        batch_pos = step_num - lag_steps + section_index
        is_valid = (batch_pos >= 0) & (batch_pos < micro_count)
        batch_slot = jnp.clip(batch_pos, 0, micro_count - 1)
        upstream = jnp.where(
            is_last, lax.dynamic_index_in_dim(loss_grad, batch_slot, 0, keepdims=False), incoming
        )
        inputs = lax.dynamic_index_in_dim(saved_in, batch_slot, 0, keepdims=False)
        grad_input = lax.cond(is_valid, run_backward, skip_backward, (inputs, upstream))
        saved_upstream = store_slot(saved_upstream, batch_slot, is_valid, upstream[:, :block_size])
        passed = shifted(grad_input, "section", -1)
        return (passed, saved_upstream)

    forward_init = (empty_rows, empty_buf, empty_head, empty_buf)
    backward_init = (empty_rows, empty_head)

    def forward_step(forward_state, step_num):
        return (forward_part(forward_state, step_num), None)

    forward_state, ignored = lax.scan(
        forward_step, forward_init, jnp.arange(sections + micro_count - 1, dtype=jnp.int32)
    )

    def backward_step(backward_state, step_num):
        return (backward_part(backward_state, forward_state[1], step_num, sections - 1), None)

    backward_state, ignored = lax.scan(
        backward_step, backward_init, jnp.arange(sections + micro_count - 1, dtype=jnp.int32)
    )
    row_total = micro_count * row_count
    left_rows = forward_state[2].reshape(row_total, block_size)
    right_rows = backward_state[1].reshape(row_total, block_size)
    left_term = lax.dot_general(
        left_rows, right_rows, (((0,), (0,)), ((), ())), preferred_element_type=jnp.float32
    )
    left_term = left_term.astype(jnp.bfloat16)
    left_total = lax.psum(left_term, "dp").astype(jnp.float32)
    share_rows = block_size // lax.axis_size("dp")
    first_row = lax.axis_index("dp") * share_rows
    left_shard = lax.dynamic_slice_in_dim(left_total, first_row, share_rows, 0)
    return (forward_state[3][None], left_shard[None])


def solution(mesh):
    in_specs = (
        P(None, "dp", None),
        P(None, "dp", None),
        P("section", None),
        P("section", None),
        P("section", "dp", None),
        P("section", "dp", None),
    )
    out_specs = (P("section", None, "dp", None), P("section", "dp", None))
    return jax.shard_map(
        per_device, mesh=mesh, in_specs=in_specs, out_specs=out_specs, check_vma=False
    )
```

profile of v0, /device:TPU:1, one launch (start us, length us, event | category | flops | bytes accessed | tf_op | source)
XLA Modules:
  0.0 1805.4 jit_solution(8007107845714510100)
XLA Ops:
  9.5 11.8 scatter_custom_fusion
  21.3 61.1 %all-gather.5.cloned.1.call-done = bf16[1,3072,768]{2,1,0:T(8,128)(2,1)} async-done(((bf16[1,96,768]{2,1,0:T(8,128)(2,1)}), bf16[1,3072,768]{2,1,0:T(8,128)(2,1)}) %all-gather.5.cloned.1.call-update) | async-done | bytes 4718608 | tf_op jit(solution)/shard_map/all_gather | solution.py:82
  82.3 67.5 %all-gather.7.cloned.1.call-done = bf16[1,3072,768]{2,1,0:T(8,128)(2,1)} async-done(((bf16[1,96,768]{2,1,0:T(8,128)(2,1)}), bf16[1,3072,768]{2,1,0:T(8,128)(2,1)}) %all-gather.7.cloned.1.call-update) | async-done | bytes 4718608 | tf_op jit(solution)/shard_map/all_gather | solution.py:83
  152.1 506.2 %while.30 = (s32[]{:T(128)}, bf16[24,3072]{1,0:T(8,128)(2,1)S(1)}, bf16[6,24,3072]{2,1,0:T(8,128)(2,1)S(1)}, bf16[6,24,768]{1,2,0:T(8,128)(2,1)}, bf16[6,24,3072...) while((s32[]{:T(128)}, bf16[24,3072]{1,0:T(8,128)(2,1)S(1)}, ...), condition=%wide.region_4.6_spmd, body=%wide.region_0.5_spmd.sunk | while | flops 227721248 | bytes 15824611 | solution.py:146
  154.4 19.3 %conditional.4 = (bf16[24,3072]{1,0:T(8,128)(2,1)S(1)}, bf16[24,768]{0,1:T(8,128)(2,1)S(1)}) conditional(s32[]{:T(128)} %convert_element_type.97, () %tuple.71, (bf16[24,3072]{1,0:T(8,128)(2,1)S(1)}, f32[1,3072]{1,0:T(1,128)S(1)}, bf16[3072,768]{1,0:T(8,128)(2,1)}, s32[3072]{0:T(1024)S(1)}, bf16[3072,768]{1,0:T(8,128)(2,1)}) %tuple.72), branch_computations={%region_1.1_spmd, %region_2.4_spmd} | conditional | flops 227481632 | bytes 13120912 | solution.py:119
  180.6 19.3 %conditional.4 = (bf16[24,3072]{1,0:T(8,128)(2,1)S(1)}, bf16[24,768]{0,1:T(8,128)(2,1)S(1)}) conditional(s32[]{:T(128)} %convert_element_type.97, () %tuple.71, (bf16[24,3072]{1,0:T(8,128)(2,1)S(1)}, f32[1,3072]{1,0:T(1,128)S(1)}, bf16[3072,768]{1,0:T(8,128)(2,1)}, s32[3072]{0:T(1024)S(1)}, bf16[3072,768]{1,0:T(8,128)(2,1)}) %tuple.72), branch_computations={%region_1.1_spmd, %region_2.4_spmd} | conditional | flops 227481632 | bytes 13120912 | solution.py:119
  213.5 19.3 %conditional.4 = (bf16[24,3072]{1,0:T(8,128)(2,1)S(1)}, bf16[24,768]{0,1:T(8,128)(2,1)S(1)}) conditional(s32[]{:T(128)} %convert_element_type.97, () %tuple.71, (bf16[24,3072]{1,0:T(8,128)(2,1)S(1)}, f32[1,3072]{1,0:T(1,128)S(1)}, bf16[3072,768]{1,0:T(8,128)(2,1)}, s32[3072]{0:T(1024)S(1)}, bf16[3072,768]{1,0:T(8,128)(2,1)}) %tuple.72), branch_computations={%region_1.1_spmd, %region_2.4_spmd} | conditional | flops 227481632 | bytes 13120912 | solution.py:119
  245.3 19.3 %conditional.4 = (bf16[24,3072]{1,0:T(8,128)(2,1)S(1)}, bf16[24,768]{0,1:T(8,128)(2,1)S(1)}) conditional(s32[]{:T(128)} %convert_element_type.97, () %tuple.71, (bf16[24,3072]{1,0:T(8,128)(2,1)S(1)}, f32[1,3072]{1,0:T(1,128)S(1)}, bf16[3072,768]{1,0:T(8,128)(2,1)}, s32[3072]{0:T(1024)S(1)}, bf16[3072,768]{1,0:T(8,128)(2,1)}) %tuple.72), branch_computations={%region_1.1_spmd, %region_2.4_spmd} | conditional | flops 227481632 | bytes 13120912 | solution.py:119
  276.7 19.3 %conditional.4 = (bf16[24,3072]{1,0:T(8,128)(2,1)S(1)}, bf16[24,768]{0,1:T(8,128)(2,1)S(1)}) conditional(s32[]{:T(128)} %convert_element_type.97, () %tuple.71, (bf16[24,3072]{1,0:T(8,128)(2,1)S(1)}, f32[1,3072]{1,0:T(1,128)S(1)}, bf16[3072,768]{1,0:T(8,128)(2,1)}, s32[3072]{0:T(1024)S(1)}, bf16[3072,768]{1,0:T(8,128)(2,1)}) %tuple.72), branch_computations={%region_1.1_spmd, %region_2.4_spmd} | conditional | flops 227481632 | bytes 13120912 | solution.py:119
  308.2 19.3 %conditional.4 = (bf16[24,3072]{1,0:T(8,128)(2,1)S(1)}, bf16[24,768]{0,1:T(8,128)(2,1)S(1)}) conditional(s32[]{:T(128)} %convert_element_type.97, () %tuple.71, (bf16[24,3072]{1,0:T(8,128)(2,1)S(1)}, f32[1,3072]{1,0:T(1,128)S(1)}, bf16[3072,768]{1,0:T(8,128)(2,1)}, s32[3072]{0:T(1024)S(1)}, bf16[3072,768]{1,0:T(8,128)(2,1)}) %tuple.72), branch_computations={%region_1.1_spmd, %region_2.4_spmd} | conditional | flops 227481632 | bytes 13120912 | solution.py:119
  339.7 25.7 %collective-permute-start = (bf16[24,3072]{1,0:T(8,128)(2,1)S(1)}, bf16[24,3072]{1,0:T(8,128)(2,1)S(1)}, u32[]{:S(2)}, u32[]{:S(2)}) collective-permute-start(bf16[24,3072]{1,0:T(8,128)(2,1)S(1)} %get-tuple-element.514), channel_id=1, source_target_pairs={{0,32},{32,64},{64,96},{96,128},{128,160},{160,192},{192,224},{224... | collective-permute-start | bytes 442376 | tf_op jit(solution)/shard_map/while/body/eval_jaxpr/ppermute | solution.py:12
  383.5 26.6 %collective-permute-start = (bf16[24,3072]{1,0:T(8,128)(2,1)S(1)}, bf16[24,3072]{1,0:T(8,128)(2,1)S(1)}, u32[]{:S(2)}, u32[]{:S(2)}) collective-permute-start(bf16[24,3072]{1,0:T(8,128)(2,1)S(1)} %get-tuple-element.514), channel_id=1, source_target_pairs={{0,32},{32,64},{64,96},{96,128},{128,160},{160,192},{192,224},{224... | collective-permute-start | bytes 442376 | tf_op jit(solution)/shard_map/while/body/eval_jaxpr/ppermute | solution.py:12
  428.9 20.3 %collective-permute-start = (bf16[24,3072]{1,0:T(8,128)(2,1)S(1)}, bf16[24,3072]{1,0:T(8,128)(2,1)S(1)}, u32[]{:S(2)}, u32[]{:S(2)}) collective-permute-start(bf16[24,3072]{1,0:T(8,128)(2,1)S(1)} %get-tuple-element.514), channel_id=1, source_target_pairs={{0,32},{32,64},{64,96},{96,128},{128,160},{160,192},{192,224},{224... | collective-permute-start | bytes 442376 | tf_op jit(solution)/shard_map/while/body/eval_jaxpr/ppermute | solution.py:12
  467.9 21.2 %collective-permute-start = (bf16[24,3072]{1,0:T(8,128)(2,1)S(1)}, bf16[24,3072]{1,0:T(8,128)(2,1)S(1)}, u32[]{:S(2)}, u32[]{:S(2)}) collective-permute-start(bf16[24,3072]{1,0:T(8,128)(2,1)S(1)} %get-tuple-element.514), channel_id=1, source_target_pairs={{0,32},{32,64},{64,96},{96,128},{128,160},{160,192},{192,224},{224... | collective-permute-start | bytes 442376 | tf_op jit(solution)/shard_map/while/body/eval_jaxpr/ppermute | solution.py:12
  507.8 21.1 %collective-permute-start = (bf16[24,3072]{1,0:T(8,128)(2,1)S(1)}, bf16[24,3072]{1,0:T(8,128)(2,1)S(1)}, u32[]{:S(2)}, u32[]{:S(2)}) collective-permute-start(bf16[24,3072]{1,0:T(8,128)(2,1)S(1)} %get-tuple-element.514), channel_id=1, source_target_pairs={{0,32},{32,64},{64,96},{96,128},{128,160},{160,192},{192,224},{224... | collective-permute-start | bytes 442376 | tf_op jit(solution)/shard_map/while/body/eval_jaxpr/ppermute | solution.py:12
  534.6 9.4 collective-permute-start
  549.8 22.0 %collective-permute-start = (bf16[24,3072]{1,0:T(8,128)(2,1)S(1)}, bf16[24,3072]{1,0:T(8,128)(2,1)S(1)}, u32[]{:S(2)}, u32[]{:S(2)}) collective-permute-start(bf16[24,3072]{1,0:T(8,128)(2,1)S(1)} %get-tuple-element.514), channel_id=1, source_target_pairs={{0,32},{32,64},{64,96},{96,128},{128,160},{160,192},{192,224},{224... | collective-permute-start | bytes 442376 | tf_op jit(solution)/shard_map/while/body/eval_jaxpr/ppermute | solution.py:12
  577.5 9.6 collective-permute-start
  592.8 22.4 %collective-permute-start = (bf16[24,3072]{1,0:T(8,128)(2,1)S(1)}, bf16[24,3072]{1,0:T(8,128)(2,1)S(1)}, u32[]{:S(2)}, u32[]{:S(2)}) collective-permute-start(bf16[24,3072]{1,0:T(8,128)(2,1)S(1)} %get-tuple-element.514), channel_id=1, source_target_pairs={{0,32},{32,64},{64,96},{96,128},{128,160},{160,192},{192,224},{224... | collective-permute-start | bytes 442376 | tf_op jit(solution)/shard_map/while/body/eval_jaxpr/ppermute | solution.py:12
  635.2 19.7 %collective-permute-start = (bf16[24,3072]{1,0:T(8,128)(2,1)S(1)}, bf16[24,3072]{1,0:T(8,128)(2,1)S(1)}, u32[]{:S(2)}, u32[]{:S(2)}) collective-permute-start(bf16[24,3072]{1,0:T(8,128)(2,1)S(1)} %get-tuple-element.514), channel_id=1, source_target_pairs={{0,32},{32,64},{64,96},{96,128},{128,160},{160,192},{192,224},{224... | collective-permute-start | bytes 442376 | tf_op jit(solution)/shard_map/while/body/eval_jaxpr/ppermute | solution.py:12
  658.3 810.8 %while.31 = (s32[]{:T(128)}, bf16[24,3072]{1,0:T(8,128)(2,1)S(1)}, bf16[6,24,768]{2,1,0:T(8,128)(2,1)S(1)}, s32[21]{0:T(128)S(1)}, s32[]{:T(128)}, /*index=5*/pr...) while((s32[]{:T(128)}, bf16[24,3072]{1,0:T(8,128)(2,1)S(1)}, ...), condition=%wide.region_11.13_spmd, body=%wide.region_6.12_spmd.sunk | while | flops 227942480 | bytes 15207745 | solution.py:153
  661.9 9.9 collective-permute-done.1
  675.4 25.0 %collective-permute-done.1 = bf16[24,3072]{1,0:T(8,128)(2,1)S(1)} collective-permute-done((bf16[24,3072]{1,0:T(8,128)(2,1)S(1)}, bf16[24,3072]{1,0:T(8,128)(2,1)S(1)}, u32[]{:S(2)}, u32[]{:S(2)}) %collective-permute-start.1) | collective-permute-done | bytes 147488 | tf_op jit(solution)/shard_map/while/body/eval_jaxpr/ppermute | solution.py:12
  703.9 14.2 collective-permute-done.1
  721.7 16.7 collective-permute-done.1
  741.9 14.0 collective-permute-done.1
  759.5 18.9 %collective-permute-done.1 = bf16[24,3072]{1,0:T(8,128)(2,1)S(1)} collective-permute-done((bf16[24,3072]{1,0:T(8,128)(2,1)S(1)}, bf16[24,3072]{1,0:T(8,128)(2,1)S(1)}, u32[]{:S(2)}, u32[]{:S(2)}) %collective-permute-start.1) | collective-permute-done | bytes 147488 | tf_op jit(solution)/shard_map/while/body/eval_jaxpr/ppermute | solution.py:12
  782.0 11.2 collective-permute-done.1
  796.8 22.4 %collective-permute-done.1 = bf16[24,3072]{1,0:T(8,128)(2,1)S(1)} collective-permute-done((bf16[24,3072]{1,0:T(8,128)(2,1)S(1)}, bf16[24,3072]{1,0:T(8,128)(2,1)S(1)}, u32[]{:S(2)}, u32[]{:S(2)}) %collective-permute-start.1) | collective-permute-done | bytes 147488 | tf_op jit(solution)/shard_map/while/body/eval_jaxpr/ppermute | solution.py:12
  822.8 11.6 collective-permute-done.1
  837.9 21.7 %collective-permute-done.1 = bf16[24,3072]{1,0:T(8,128)(2,1)S(1)} collective-permute-done((bf16[24,3072]{1,0:T(8,128)(2,1)S(1)}, bf16[24,3072]{1,0:T(8,128)(2,1)S(1)}, u32[]{:S(2)}, u32[]{:S(2)}) %collective-permute-start.1) | collective-permute-done | bytes 147488 | tf_op jit(solution)/shard_map/while/body/eval_jaxpr/ppermute | solution.py:12
  863.2 11.2 collective-permute-done.1
  878.0 25.5 %collective-permute-done.1 = bf16[24,3072]{1,0:T(8,128)(2,1)S(1)} collective-permute-done((bf16[24,3072]{1,0:T(8,128)(2,1)S(1)}, bf16[24,3072]{1,0:T(8,128)(2,1)S(1)}, u32[]{:S(2)}, u32[]{:S(2)}) %collective-permute-start.1) | collective-permute-done | bytes 147488 | tf_op jit(solution)/shard_map/while/body/eval_jaxpr/ppermute | solution.py:12
  919.6 28.9 %collective-permute-done.1 = bf16[24,3072]{1,0:T(8,128)(2,1)S(1)} collective-permute-done((bf16[24,3072]{1,0:T(8,128)(2,1)S(1)}, bf16[24,3072]{1,0:T(8,128)(2,1)S(1)}, u32[]{:S(2)}, u32[]{:S(2)}) %collective-permute-start.1) | collective-permute-done | bytes 147488 | tf_op jit(solution)/shard_map/while/body/eval_jaxpr/ppermute | solution.py:12
  952.0 304.7 %collective-permute-done.1 = bf16[24,3072]{1,0:T(8,128)(2,1)S(1)} collective-permute-done((bf16[24,3072]{1,0:T(8,128)(2,1)S(1)}, bf16[24,3072]{1,0:T(8,128)(2,1)S(1)}, u32[]{:S(2)}, u32[]{:S(2)}) %collective-permute-start.1) | collective-permute-done | bytes 147488 | tf_op jit(solution)/shard_map/while/body/eval_jaxpr/ppermute | solution.py:12
  1258.9 20.4 %conditional.5 = (bf16[24,3072]{1,0:T(8,128)(2,1)S(1)}) conditional(s32[]{:T(128)} %convert_element_type.98, () %tuple.74, (bf16[24,3072]{1,0:T(8,128)(2,1)S(1)}, bf16[6,24,3072]{2,1,0:T(8,128)(2,1)S(1)}, s32[]{:T(128)}, bf16[3072,768]{1,0:T(8,128)(2,1)}, s32[3072]{0:T(1024)S(1)}, /*index=5*/bf16[3072,768]{1,0:T(8,128)(2,1)}, ...), branch_computations={%region_7.8_spmd, %region_8.11_spmd} | conditional | flops 227850304 | bytes 13990880 | solution.py:135
  1263.2 9.2 gather_fusion
  1280.7 13.5 collective-permute-done.1
  1296.3 20.4 %conditional.5 = (bf16[24,3072]{1,0:T(8,128)(2,1)S(1)}) conditional(s32[]{:T(128)} %convert_element_type.98, () %tuple.74, (bf16[24,3072]{1,0:T(8,128)(2,1)S(1)}, bf16[6,24,3072]{2,1,0:T(8,128)(2,1)S(1)}, s32[]{:T(128)}, bf16[3072,768]{1,0:T(8,128)(2,1)}, s32[3072]{0:T(1024)S(1)}, /*index=5*/bf16[3072,768]{1,0:T(8,128)(2,1)}, ...), branch_computations={%region_7.8_spmd, %region_8.11_spmd} | conditional | flops 227850304 | bytes 13990880 | solution.py:135
  1318.1 15.1 collective-permute-done.1
  1335.4 20.4 %conditional.5 = (bf16[24,3072]{1,0:T(8,128)(2,1)S(1)}) conditional(s32[]{:T(128)} %convert_element_type.98, () %tuple.74, (bf16[24,3072]{1,0:T(8,128)(2,1)S(1)}, bf16[6,24,3072]{2,1,0:T(8,128)(2,1)S(1)}, s32[]{:T(128)}, bf16[3072,768]{1,0:T(8,128)(2,1)}, s32[3072]{0:T(1024)S(1)}, /*index=5*/bf16[3072,768]{1,0:T(8,128)(2,1)}, ...), branch_computations={%region_7.8_spmd, %region_8.11_spmd} | conditional | flops 227850304 | bytes 13990880 | solution.py:135
  1357.1 12.9 collective-permute-done.1
  1372.2 20.4 %conditional.5 = (bf16[24,3072]{1,0:T(8,128)(2,1)S(1)}) conditional(s32[]{:T(128)} %convert_element_type.98, () %tuple.74, (bf16[24,3072]{1,0:T(8,128)(2,1)S(1)}, bf16[6,24,3072]{2,1,0:T(8,128)(2,1)S(1)}, s32[]{:T(128)}, bf16[3072,768]{1,0:T(8,128)(2,1)}, s32[3072]{0:T(1024)S(1)}, /*index=5*/bf16[3072,768]{1,0:T(8,128)(2,1)}, ...), branch_computations={%region_7.8_spmd, %region_8.11_spmd} | conditional | flops 227850304 | bytes 13990880 | solution.py:135
  1393.9 9.3 collective-permute-done.1
  1405.5 20.4 %conditional.5 = (bf16[24,3072]{1,0:T(8,128)(2,1)S(1)}) conditional(s32[]{:T(128)} %convert_element_type.98, () %tuple.74, (bf16[24,3072]{1,0:T(8,128)(2,1)S(1)}, bf16[6,24,3072]{2,1,0:T(8,128)(2,1)S(1)}, s32[]{:T(128)}, bf16[3072,768]{1,0:T(8,128)(2,1)}, s32[3072]{0:T(1024)S(1)}, /*index=5*/bf16[3072,768]{1,0:T(8,128)(2,1)}, ...), branch_computations={%region_7.8_spmd, %region_8.11_spmd} | conditional | flops 227850304 | bytes 13990880 | solution.py:135
  1427.2 9.3 collective-permute-done.1
  1438.8 20.4 %conditional.5 = (bf16[24,3072]{1,0:T(8,128)(2,1)S(1)}) conditional(s32[]{:T(128)} %convert_element_type.98, () %tuple.74, (bf16[24,3072]{1,0:T(8,128)(2,1)S(1)}, bf16[6,24,3072]{2,1,0:T(8,128)(2,1)S(1)}, s32[]{:T(128)}, bf16[3072,768]{1,0:T(8,128)(2,1)}, s32[3072]{0:T(1024)S(1)}, /*index=5*/bf16[3072,768]{1,0:T(8,128)(2,1)}, ...), branch_computations={%region_7.8_spmd, %region_8.11_spmd} | conditional | flops 227850304 | bytes 13990880 | solution.py:135
  1472.0 325.5 %all-reduce.2.cloned.1.call-done = bf16[768,768]{1,0:T(8,128)(2,1)} async-done(((bf16[768,768]{1,0:T(8,128)(2,1)}), bf16[768,768]{1,0:T(8,128)(2,1)}) %all-reduce.2.cloned.1.call-update) | async-done | bytes 1179664 | tf_op jit(solution)/shard_map/psum | solution.py:163
  (562 shorter events, 493.0 us)
Async XLA Ops:
  7.2 144.9 %copy-start.1 = (s32[1,3072]{1,0:T(1,128)S(1)}, s32[1,3072]{1,0:T(1,128)}, u32[]{:S(2)}) copy-start(s32[1,3072]{1,0:T(1,128)} %param.19) | copy-start | bytes 36868
  7.2 144.9 %copy-start = (f32[1,3072]{1,0:T(1,128)S(1)}, f32[1,3072]{1,0:T(1,128)}, u32[]{:S(2)}) copy-start(f32[1,3072]{1,0:T(1,128)} %param.18) | copy-start | bytes 36868
  7.2 75.2 %all-gather.5.cloned.1.call-start = ((), (), s32[]{:S(2)}) async-start(), calls=%async_computation.1 | async-start | bytes 4866048 | tf_op jit(solution)/shard_map/all_gather | solution.py:82
  7.9 141.9 %all-gather.7.cloned.1.call-start = ((), (), s32[]{:S(2)}) async-start(), calls=%async_computation.2 | async-start | bytes 4866048 | tf_op jit(solution)/shard_map/all_gather | solution.py:83
  8.7 1788.8 %all-reduce.2.cloned.1.call-start = ((), (), s32[]{:S(2)}) async-start(), calls=%async_computation | async-start | bytes 2359296 | tf_op jit(solution)/shard_map/psum | solution.py:163
  173.7 4.6 collective-permute-start
  200.0 11.2 collective-permute-start
  232.8 10.2 collective-permute-start
  264.7 9.8 collective-permute-start
  296.1 9.8 collective-permute-start
  327.5 9.8 collective-permute-start
  339.7 29.1 %collective-permute-start = (bf16[24,3072]{1,0:T(8,128)(2,1)S(1)}, bf16[24,3072]{1,0:T(8,128)(2,1)S(1)}, u32[]{:S(2)}, u32[]{:S(2)}) collective-permute-start(bf16[24,3072]{1,0:T(8,128)(2,1)S(1)} %get-tuple-element.514), channel_id=1, source_target_pairs={{0,32},{32,64},{64,96},{96,128},{128,160},{160,192},{192,224},{224... | collective-permute-start | bytes 442376 | tf_op jit(solution)/shard_map/while/body/eval_jaxpr/ppermute | solution.py:12
  371.1 10.0 collective-permute-start
  383.5 30.0 %collective-permute-start = (bf16[24,3072]{1,0:T(8,128)(2,1)S(1)}, bf16[24,3072]{1,0:T(8,128)(2,1)S(1)}, u32[]{:S(2)}, u32[]{:S(2)}) collective-permute-start(bf16[24,3072]{1,0:T(8,128)(2,1)S(1)} %get-tuple-element.514), channel_id=1, source_target_pairs={{0,32},{32,64},{64,96},{96,128},{128,160},{160,192},{192,224},{224... | collective-permute-start | bytes 442376 | tf_op jit(solution)/shard_map/while/body/eval_jaxpr/ppermute | solution.py:12
  415.8 10.7 collective-permute-start
  428.9 23.6 %collective-permute-start = (bf16[24,3072]{1,0:T(8,128)(2,1)S(1)}, bf16[24,3072]{1,0:T(8,128)(2,1)S(1)}, u32[]{:S(2)}, u32[]{:S(2)}) collective-permute-start(bf16[24,3072]{1,0:T(8,128)(2,1)S(1)} %get-tuple-element.514), channel_id=1, source_target_pairs={{0,32},{32,64},{64,96},{96,128},{128,160},{160,192},{192,224},{224... | collective-permute-start | bytes 442376 | tf_op jit(solution)/shard_map/while/body/eval_jaxpr/ppermute | solution.py:12
  454.8 10.7 collective-permute-start
  467.9 24.5 %collective-permute-start = (bf16[24,3072]{1,0:T(8,128)(2,1)S(1)}, bf16[24,3072]{1,0:T(8,128)(2,1)S(1)}, u32[]{:S(2)}, u32[]{:S(2)}) collective-permute-start(bf16[24,3072]{1,0:T(8,128)(2,1)S(1)} %get-tuple-element.514), channel_id=1, source_target_pairs={{0,32},{32,64},{64,96},{96,128},{128,160},{160,192},{192,224},{224... | collective-permute-start | bytes 442376 | tf_op jit(solution)/shard_map/while/body/eval_jaxpr/ppermute | solution.py:12
  494.8 10.7 collective-permute-start
  507.8 24.5 %collective-permute-start = (bf16[24,3072]{1,0:T(8,128)(2,1)S(1)}, bf16[24,3072]{1,0:T(8,128)(2,1)S(1)}, u32[]{:S(2)}, u32[]{:S(2)}) collective-permute-start(bf16[24,3072]{1,0:T(8,128)(2,1)S(1)} %get-tuple-element.514), channel_id=1, source_target_pairs={{0,32},{32,64},{64,96},{96,128},{128,160},{160,192},{192,224},{224... | collective-permute-start | bytes 442376 | tf_op jit(solution)/shard_map/while/body/eval_jaxpr/ppermute | solution.py:12
  534.6 12.8 collective-permute-start
  549.8 25.4 %collective-permute-start = (bf16[24,3072]{1,0:T(8,128)(2,1)S(1)}, bf16[24,3072]{1,0:T(8,128)(2,1)S(1)}, u32[]{:S(2)}, u32[]{:S(2)}) collective-permute-start(bf16[24,3072]{1,0:T(8,128)(2,1)S(1)} %get-tuple-element.514), channel_id=1, source_target_pairs={{0,32},{32,64},{64,96},{96,128},{128,160},{160,192},{192,224},{224... | collective-permute-start | bytes 442376 | tf_op jit(solution)/shard_map/while/body/eval_jaxpr/ppermute | solution.py:12
  577.5 13.0 collective-permute-start
  592.8 25.8 %collective-permute-start = (bf16[24,3072]{1,0:T(8,128)(2,1)S(1)}, bf16[24,3072]{1,0:T(8,128)(2,1)S(1)}, u32[]{:S(2)}, u32[]{:S(2)}) collective-permute-start(bf16[24,3072]{1,0:T(8,128)(2,1)S(1)} %get-tuple-element.514), channel_id=1, source_target_pairs={{0,32},{32,64},{64,96},{96,128},{128,160},{160,192},{192,224},{224... | collective-permute-start | bytes 442376 | tf_op jit(solution)/shard_map/while/body/eval_jaxpr/ppermute | solution.py:12
  621.0 11.9 collective-permute-start
  635.2 23.1 %collective-permute-start = (bf16[24,3072]{1,0:T(8,128)(2,1)S(1)}, bf16[24,3072]{1,0:T(8,128)(2,1)S(1)}, u32[]{:S(2)}, u32[]{:S(2)}) collective-permute-start(bf16[24,3072]{1,0:T(8,128)(2,1)S(1)} %get-tuple-element.514), channel_id=1, source_target_pairs={{0,32},{32,64},{64,96},{96,128},{128,160},{160,192},{192,224},{224... | collective-permute-start | bytes 442376 | tf_op jit(solution)/shard_map/while/body/eval_jaxpr/ppermute | solution.py:12
  660.5 11.3 collective-permute-start.1
  674.0 26.3 %collective-permute-start.1 = (bf16[24,3072]{1,0:T(8,128)(2,1)S(1)}, bf16[24,3072]{1,0:T(8,128)(2,1)S(1)}, u32[]{:S(2)}, u32[]{:S(2)}) collective-permute-start(bf16[24,3072]{1,0:T(8,128)(2,1)S(1)} %get-tuple-element.635), channel_id=1, source_target_pairs={{32,0},{64,32},{96,64},{128,96},{160,128},{192,160},{224,192},{256... | collective-permute-start | bytes 442376 | tf_op jit(solution)/shard_map/while/body/eval_jaxpr/ppermute | solution.py:12
  702.6 15.5 collective-permute-start.1
  720.3 18.0 collective-permute-start.1
  740.6 15.4 collective-permute-start.1
  758.2 20.3 %collective-permute-start.1 = (bf16[24,3072]{1,0:T(8,128)(2,1)S(1)}, bf16[24,3072]{1,0:T(8,128)(2,1)S(1)}, u32[]{:S(2)}, u32[]{:S(2)}) collective-permute-start(bf16[24,3072]{1,0:T(8,128)(2,1)S(1)} %get-tuple-element.635), channel_id=1, source_target_pairs={{32,0},{64,32},{96,64},{128,96},{160,128},{192,160},{224,192},{256... | collective-permute-start | bytes 442376 | tf_op jit(solution)/shard_map/while/body/eval_jaxpr/ppermute | solution.py:12
  780.7 12.5 collective-permute-start.1
  795.4 23.7 %collective-permute-start.1 = (bf16[24,3072]{1,0:T(8,128)(2,1)S(1)}, bf16[24,3072]{1,0:T(8,128)(2,1)S(1)}, u32[]{:S(2)}, u32[]{:S(2)}) collective-permute-start(bf16[24,3072]{1,0:T(8,128)(2,1)S(1)} %get-tuple-element.635), channel_id=1, source_target_pairs={{32,0},{64,32},{96,64},{128,96},{160,128},{192,160},{224,192},{256... | collective-permute-start | bytes 442376 | tf_op jit(solution)/shard_map/while/body/eval_jaxpr/ppermute | solution.py:12
  821.4 12.9 collective-permute-start.1
  836.6 23.1 %collective-permute-start.1 = (bf16[24,3072]{1,0:T(8,128)(2,1)S(1)}, bf16[24,3072]{1,0:T(8,128)(2,1)S(1)}, u32[]{:S(2)}, u32[]{:S(2)}) collective-permute-start(bf16[24,3072]{1,0:T(8,128)(2,1)S(1)} %get-tuple-element.635), channel_id=1, source_target_pairs={{32,0},{64,32},{96,64},{128,96},{160,128},{192,160},{224,192},{256... | collective-permute-start | bytes 442376 | tf_op jit(solution)/shard_map/while/body/eval_jaxpr/ppermute | solution.py:12
  861.9 12.5 collective-permute-start.1
  876.6 26.9 %collective-permute-start.1 = (bf16[24,3072]{1,0:T(8,128)(2,1)S(1)}, bf16[24,3072]{1,0:T(8,128)(2,1)S(1)}, u32[]{:S(2)}, u32[]{:S(2)}) collective-permute-start(bf16[24,3072]{1,0:T(8,128)(2,1)S(1)} %get-tuple-element.635), channel_id=1, source_target_pairs={{32,0},{64,32},{96,64},{128,96},{160,128},{192,160},{224,192},{256... | collective-permute-start | bytes 442376 | tf_op jit(solution)/shard_map/while/body/eval_jaxpr/ppermute | solution.py:12
  905.7 10.3 collective-permute-start.1
  918.2 30.2 %collective-permute-start.1 = (bf16[24,3072]{1,0:T(8,128)(2,1)S(1)}, bf16[24,3072]{1,0:T(8,128)(2,1)S(1)}, u32[]{:S(2)}, u32[]{:S(2)}) collective-permute-start(bf16[24,3072]{1,0:T(8,128)(2,1)S(1)} %get-tuple-element.635), channel_id=1, source_target_pairs={{32,0},{64,32},{96,64},{128,96},{160,128},{192,160},{224,192},{256... | collective-permute-start | bytes 442376 | tf_op jit(solution)/shard_map/while/body/eval_jaxpr/ppermute | solution.py:12
  950.7 306.0 %collective-permute-start.1 = (bf16[24,3072]{1,0:T(8,128)(2,1)S(1)}, bf16[24,3072]{1,0:T(8,128)(2,1)S(1)}, u32[]{:S(2)}, u32[]{:S(2)}) collective-permute-start(bf16[24,3072]{1,0:T(8,128)(2,1)S(1)} %get-tuple-element.635), channel_id=1, source_target_pairs={{32,0},{64,32},{96,64},{128,96},{160,128},{192,160},{224,192},{256... | collective-permute-start | bytes 442376 | tf_op jit(solution)/shard_map/while/body/eval_jaxpr/ppermute | solution.py:12
  1279.3 14.8 collective-permute-start.1
  1316.7 16.4 collective-permute-start.1
  1355.8 14.2 collective-permute-start.1
  1392.6 10.7 collective-permute-start.1
  1425.9 10.7 collective-permute-start.1
  1459.2 9.9 collective-permute-start.1
Sparse Core Ops, SparseCore 0:
  10.1 72.1 all-gather.4
  84.5 65.2 all-gather.6
  1472.1 325.2 all-reduce.1
where the time goes:
time: 1810 us
  waiting for transfers between devices  1070 us (59%)
  starting transfers between devices  298 us (16%)
  local copies, waits for them, and re-layouts  199 us (11%)
  other arithmetic  110 us (6%)
  matrix products  84.7 us (5%)
  loops' own time  30.9 us (2%)
    ppermute x42, waiting for transfers between devices, shifted(): return lax.ppermute(array, axis, pairs)  614 us
    psum x1, waiting for transfers between devices, per_device(): left_total = lax.psum(left_term, 'dp').astype(jnp.float32)  325 us
    ppermute x42, starting transfers between devices, shifted(): return lax.ppermute(array, axis, pairs)  298 us
    all_gather x1, waiting for transfers between devices, per_device(): lax.all_gather(left_factor[0], 'dp', axis=0, tiled=True)  67.5 us
    all_gather x1, waiting for transfers between devices, per_device(): lax.all_gather(right_factor[0], 'dp', axis=0, tiled=True)  61.1 us
    gather x6, local copies, waits for them, and re-layouts, layer_backward(): before = jnp.take(through, inverse, axis=1)  55 us
    gather x6, local copies, waits for them, and re-layouts, layer_forward(): permuted = jnp.take(mixed, shuffle, axis=1)  55 us
    dynamic_update_slice x84, other arithmetic, store_slot(): lax.dynamic_update_index_in_dim(buffer, jnp.where(is_valid, new_value, ol...  51.4 us
  transfers between devices with their start and end apart: 45, of which 24 were waited for; matrix products, arithmetic and copies ran while one was open for 5% of the time, Pallas kernels for 0%

commit v1 on v0

v1 whole, which is shorter than its diff:
```python
import jax
import jax.numpy as jnp
from jax import lax
from jax.experimental import pallas as pl
from jax.sharding import PartitionSpec as P

epsilon = 1e-05


def shifted(array, axis, by):
    peers = lax.axis_size(axis)
    pairs = [(i, i + by) for i in range(peers) if 0 <= i + by < peers]
    return lax.ppermute(array, axis, pairs)


def whole_kernel(right_ref, rows_ref, owner_ref, gain_ref, whole_ref):
    column_block = pl.program_id(1)
    spread = jnp.where(
        owner_ref[...] == column_block, rows_ref[...].astype(jnp.float32), 0.0
    ).astype(jnp.bfloat16)
    product = jnp.dot(right_ref[...], spread, preferred_element_type=jnp.float32)
    whole_ref[...] = (product * gain_ref[...]).astype(jnp.bfloat16)


def build_maps(gain_row, order, right_full, left_full):
    channels, block = left_full.shape
    count = channels // block
    inverse = jnp.zeros((channels,), jnp.int32).at[order].set(jnp.arange(channels, dtype=jnp.int32))
    rows = jnp.take(left_full, inverse, axis=0)
    whole = pl.pallas_call(
        whole_kernel,
        grid=(count, count),
        in_specs=[
            pl.BlockSpec((block, block), lambda n, b: (n, 0)),
            pl.BlockSpec((block, block), lambda n, b: (n, 0)),
            pl.BlockSpec((block, 1), lambda n, b: (n, 0)),
            pl.BlockSpec((block, 1), lambda n, b: (n, 0)),
        ],
        out_specs=pl.BlockSpec((block, block), lambda n, b: (n, b)),
        out_shape=jax.ShapeDtypeStruct((channels, channels), jnp.bfloat16),
        name="whole_map",
    )(right_full, rows, (inverse // block)[:, None], gain_row[:, None])
    pick = (order[None, :block] == jnp.arange(channels)[:, None]).astype(jnp.bfloat16)
    head = jnp.einsum(
        "nkj,nji->nki",
        right_full.reshape(count, block, block),
        pick.reshape(count, block, block),
        preferred_element_type=jnp.float32,
    ).astype(jnp.bfloat16).reshape(channels, block)
    return whole, head


def inverse_norm(wide_in):
    return lax.rsqrt(jnp.mean(wide_in * wide_in, axis=-1, keepdims=True) + epsilon)


def per_device(section_input, loss_grad, norm_gain, channel_order, right_factor, left_factor):
    sections = lax.axis_size("section")
    section_index = lax.axis_index("section")
    micro_count, row_count, channels = section_input.shape
    block_size = right_factor.shape[2]
    left_full = lax.all_gather(left_factor[0], "dp", axis=0, tiled=True)
    right_full = lax.all_gather(right_factor[0], "dp", axis=0, tiled=True)
    gain_row = norm_gain[0]
    whole, head = build_maps(gain_row, channel_order[0], right_full, left_full)
    is_first = section_index == 0
    is_last = section_index == sections - 1
    empty_rows = jnp.zeros((row_count, channels), jnp.bfloat16)
    empty_buf = jnp.zeros((micro_count + 1, row_count, channels), jnp.bfloat16)

    def slots(batch_pos):
        is_valid = (batch_pos >= 0) & (batch_pos < micro_count)
        return jnp.clip(batch_pos, 0, micro_count - 1), jnp.where(is_valid, batch_pos, micro_count)

    def forward_step(state, step_num):
        incoming, saved_in, outputs = state
        read, write = slots(step_num - section_index)
        inputs = jnp.where(
            is_first, lax.dynamic_index_in_dim(section_input, read, 0, keepdims=False), incoming
        )
        wide_in = inputs.astype(jnp.float32)
        product = jnp.dot(inputs, whole, preferred_element_type=jnp.float32)
        output = (wide_in + inverse_norm(wide_in) * product).astype(jnp.bfloat16)
        passed = shifted(output, "section", 1)
        saved_in = lax.dynamic_update_index_in_dim(saved_in, inputs, write, 0)
        outputs = lax.dynamic_update_index_in_dim(outputs, output, write, 0)
        return (passed, saved_in, outputs), None

    steps = jnp.arange(sections + micro_count - 1, dtype=jnp.int32)
    (_, saved_in, outputs), _ = lax.scan(forward_step, (empty_rows, empty_buf, empty_buf), steps)

    def backward_step(state, step_num):
        incoming, saved_up = state
        read, write = slots(step_num - (sections - 1) + section_index)
        upstream = jnp.where(
            is_last, lax.dynamic_index_in_dim(loss_grad, read, 0, keepdims=False), incoming
        )
        wide_in = lax.dynamic_index_in_dim(saved_in, read, 0, keepdims=False).astype(jnp.float32)
        inverse_rms = inverse_norm(wide_in)
        scaled = lax.dot_general(
            upstream, whole, (((1,), (1,)), ((), ())), preferred_element_type=jnp.float32
        )
        grad_input = (
            upstream.astype(jnp.float32)
            + inverse_rms * scaled
            - wide_in * (inverse_rms * inverse_rms * inverse_rms)
            * jnp.mean(scaled * wide_in, axis=-1, keepdims=True)
        ).astype(jnp.bfloat16)
        passed = shifted(grad_input, "section", -1)
        saved_up = lax.dynamic_update_index_in_dim(saved_up, upstream[:, :block_size], write, 0)
        return (passed, saved_up), None

    empty_head = jnp.zeros((micro_count + 1, row_count, block_size), jnp.bfloat16)
    (_, saved_up), _ = lax.scan(backward_step, (empty_rows, empty_head), steps)

    row_total = micro_count * row_count
    wide_in = saved_in[:micro_count].reshape(row_total, channels).astype(jnp.float32)
    normed = (wide_in * inverse_norm(wide_in) * gain_row).astype(jnp.bfloat16)
    permuted = jnp.dot(normed, head, preferred_element_type=jnp.float32).astype(jnp.bfloat16)
    return (outputs[None, :micro_count], left_gradient(permuted, saved_up[:micro_count].reshape(row_total, block_size))[None])


def left_gradient(left_rows, right_rows):
    peers = lax.axis_size("dp")
    block_size = left_rows.shape[1]
    term = lax.dot_general(
        left_rows, right_rows, (((0,), (0,)), ((), ())), preferred_element_type=jnp.float32
    ).astype(jnp.bfloat16)
    parts = lax.all_to_all(
        term.reshape(peers, block_size // peers, block_size), "dp", split_axis=0, concat_axis=0
    )
    return jnp.sum(parts.astype(jnp.float32), axis=0)


def solution(mesh):
    in_specs = (
        P(None, "dp", None),
        P(None, "dp", None),
        P("section", None),
        P("section", None),
        P("section", "dp", None),
        P("section", "dp", None),
    )
    out_specs = (P("section", None, "dp", None), P("section", "dp", None))
    return jax.shard_map(
        per_device, mesh=mesh, in_specs=in_specs, out_specs=out_specs, check_vma=False
    )
```

time: 1810 us -> 1270 us (0.70)
  waiting for transfers between devices: 1070 us -> 401 us
  matrix products: 84.7 us -> 390 us
  local copies, waits for them, and re-layouts: 199 us -> 60.2 us
  other arithmetic: 110 us -> 54.9 us
  Pallas kernels: 0 us -> 26.7 us
    ppermute x42, waiting for transfers between devices: 614 us -> 271 us  [shifted(): return lax.ppermute(array, axis, pairs)]
    psum x1 -> x0, waiting for transfers between devices: 325 us -> none  [per_device(): left_total = lax.psum(left_term, 'dp').astype(jnp.float32)]
    dot_general x25 -> x44, matrix products: 84.7 us -> 390 us  [the longest x21 190 us: backward_step(): lax.dot_general(upstream, whole, (((1,), (1,)), ((), ())), preferred_elem...]
    gather x12 -> x1, local copies, waits for them, and re-layouts: 110 us -> 17.7 us  [build_maps(): rows = jnp.take(left_full, inverse, axis=0)]
    ppermute x42, starting transfers between devices: 298 us -> 218 us  [shifted(): return lax.ppermute(array, axis, pairs)]
    all_to_all x0 -> x1, starting transfers between devices: none -> 66.4 us  [left_gradient(): lax.all_to_all(term.reshape(peers, block_size // peers, block_size), 'dp'...]
    dynamic_slice x126 -> x42, local copies, waits for them, and re-layouts: 65 us -> 24.5 us  [per_device(): lax.scan(forward_step, (empty_rows, empty_buf, empty_buf), steps)]
    dynamic_update_slice x84 -> x21, other arithmetic: 51.4 us -> 20 us  [forward_step(): saved_in = lax.dynamic_update_index_in_dim(saved_in, inputs, write, 0)]
  transfers between devices with their start and end apart: 45 -> 45, of which waited for: 24 -> 45; matrix products, arithmetic and copies ran while one was open for 5% -> 3% of each run, Pallas kernels for 0% -> 0%
where the time goes in v1:
time: 1270 us; the launch traced here: 1260 us
  waiting for transfers between devices  401 us (32%)
  matrix products  390 us (31%)
  starting transfers between devices  285 us (22%)
  local copies, waits for them, and re-layouts  60.2 us (5%)
  other arithmetic  54.9 us (4%)
  loops' own time  27.6 us (2%)
  Pallas kernels  26.7 us (2%)
  between operations  14.1 us (1%)
    ppermute x42, waiting for transfers between devices, shifted(): return lax.ppermute(array, axis, pairs)  271 us
    ppermute x42, starting transfers between devices, shifted(): return lax.ppermute(array, axis, pairs)  218 us
    dot_general x21, matrix products, backward_step(): lax.dot_general(upstream, whole, (((1,), (1,)), ((), ())), preferred_elem...  190 us
    dot_general x21, matrix products, forward_step(): product = jnp.dot(inputs, whole, preferred_element_type=jnp.float32)  188 us
    all_to_all x1, starting transfers between devices, left_gradient(): lax.all_to_all(term.reshape(peers, block_size // peers, block_size), 'dp'...  66.4 us
    all_gather x1, waiting for transfers between devices, per_device(): left_full = lax.all_gather(left_factor[0], 'dp', axis=0, tiled=True)  56.3 us
    all_gather x1, waiting for transfers between devices, per_device(): right_full = lax.all_gather(right_factor[0], 'dp', axis=0, tiled=True)  44.1 us
    all_to_all x1, waiting for transfers between devices, left_gradient(): lax.all_to_all(term.reshape(peers, block_size // peers, block_size), 'dp'...  28.2 us
  transfers between devices with their start and end apart: 45, of which 45 were waited for; matrix products, arithmetic and copies ran while one was open for 3% of the time, Pallas kernels for 0%

profile of v1, /device:TPU:1, one launch (start us, length us, event | category | flops | bytes accessed | tf_op | source)
XLA Modules:
  0.0 1259.7 jit_solution(6801476852575689622)
XLA Ops:
  9.4 11.8 scatter_custom_fusion
  26.0 56.3 %all-gather.7.cloned.1.call-done = bf16[1,3072,768]{2,1,0:T(8,128)(2,1)} async-done(((bf16[1,96,768]{2,1,0:T(8,128)(2,1)}), bf16[1,3072,768]{2,1,0:T(8,128)(2,1)}) %all-gather.7.cloned.1.call-update) | async-done | bytes 4718608 | tf_op jit(solution)/shard_map/all_gather | solution.py:62
  82.3 17.7 %gather_fusion = bf16[3072,768]{1,0:T(8,128)(2,1)} fusion(bf16[3072,768]{1,0:T(8,128)(2,1)} %bitcast.70, s32[3072]{0:T(1024)S(1)} %get-tuple-element.213), kind=kCustom, calls=%fused_computation | custom fusion | bytes 9449472 | tf_op jit(solution)/shard_map/jit(_take)/gather | solution.py:29
  105.7 44.1 %all-gather.5.cloned.1.call-done = bf16[1,3072,768]{2,1,0:T(8,128)(2,1)} async-done(((bf16[1,96,768]{2,1,0:T(8,128)(2,1)}), bf16[1,3072,768]{2,1,0:T(8,128)(2,1)}) %all-gather.5.cloned.1.call-update) | async-done | bytes 4718608 | tf_op jit(solution)/shard_map/all_gather | solution.py:63
  149.8 26.7 %whole_map.1 = bf16[3072,3072]{1,0:T(8,128)(2,1)} custom-call(bf16[3072,768]{1,0:T(8,128)(2,1)} %bitcast.72, bf16[3072,768]{1,0:T(8,128)(2,1)} %broadcast_select_fusion.rows_ref, s32[3072,1]{1,0:T(8,128)} %copy.8.owner_ref, f32[3072,1]{1,0:T(8,128)} %copy.9.gain_ref), custom_call_target="tpu_custom_call" | custom-call | tf_op jit(solution)/shard_map/whole_map/pallas_call | solution.py:30
  176.8 471.5 %while.28 = (s32[]{:T(128)}, bf16[24,3072]{1,0:T(8,128)(2,1)S(1)}, bf16[7,24,3072]{2,1,0:T(8,128)(2,1)S(1)}, bf16[7,24,3072]{2,1,0:T(8,128)(2,1)S(1)}, pred[]{:T...) while((s32[]{:T(128)}, bf16[24,3072]{1,0:T(8,128)(2,1)S(1)}, ...), condition=%wide.region_3.4_spmd, body=%wide.region_1.0_spmd.sunk | while | flops 453574688 | bytes 20792396 | solution.py:90
  272.1 10.4 collective-permute-start
  295.7 9.2 collective-permute-start
  362.1 9.4 collective-permute-start
  384.8 9.4 collective-permute-start
  407.5 9.4 collective-permute-start
  430.2 9.4 collective-permute-start
  452.9 9.4 collective-permute-start
  475.6 9.7 collective-permute-start
  498.6 9.8 collective-permute-start
  521.6 9.8 collective-permute-start
  544.8 9.8 collective-permute-start
  567.9 10.4 collective-permute-start
  591.6 9.1 collective-permute-start
  614.0 9.3 collective-permute-start
  636.6 9.6 collective-permute-start
  648.6 493.9 %while.29 = (s32[]{:T(128)}, bf16[24,3072]{1,0:T(8,128)(2,1)S(1)}, bf16[7,24,768]{2,1,0:T(8,128)(2,1)S(1)}, pred[]{:T(512)}, s32[21]{0:T(128)S(1)}, /*index=5*/s...) while((s32[]{:T(128)}, bf16[24,3072]{1,0:T(8,128)(2,1)S(1)}, ...), condition=%wide.region_8.9_spmd, body=%wide.region_5.8_spmd.sunk | while | flops 454017088 | bytes 21308672 | solution.py:114
  650.8 9.1 fusion.44
  661.4 10.2 collective-permute-done.1
  673.8 9.1 fusion.44
  684.3 9.8 collective-permute-done.1
  706.8 13.2 %collective-permute-done.1 = bf16[24,3072]{1,0:T(8,128)(2,1)S(1)} collective-permute-done((bf16[24,3072]{1,0:T(8,128)(2,1)S(1)}, bf16[24,3072]{1,0:T(8,128)(2,1)S(1)}, u32[]{:S(2)}, u32[]{:S(2)}) %collective-permute-start.1) | collective-permute-done | bytes 147488 | tf_op jit(solution)/shard_map/while/body/eval_jaxpr/ppermute | solution.py:13
  722.2 9.1 fusion.44
  732.8 10.5 collective-permute-done.1
  756.0 10.4 collective-permute-done.1
  779.2 11.4 collective-permute-done.1
  803.3 14.2 %collective-permute-done.1 = bf16[24,3072]{1,0:T(8,128)(2,1)S(1)} collective-permute-done((bf16[24,3072]{1,0:T(8,128)(2,1)S(1)}, bf16[24,3072]{1,0:T(8,128)(2,1)S(1)}, u32[]{:S(2)}, u32[]{:S(2)}) %collective-permute-start.1) | collective-permute-done | bytes 147488 | tf_op jit(solution)/shard_map/while/body/eval_jaxpr/ppermute | solution.py:13
  830.2 13.1 %collective-permute-done.1 = bf16[24,3072]{1,0:T(8,128)(2,1)S(1)} collective-permute-done((bf16[24,3072]{1,0:T(8,128)(2,1)S(1)}, bf16[24,3072]{1,0:T(8,128)(2,1)S(1)}, u32[]{:S(2)}, u32[]{:S(2)}) %collective-permute-start.1) | collective-permute-done | bytes 147488 | tf_op jit(solution)/shard_map/while/body/eval_jaxpr/ppermute | solution.py:13
  845.5 9.1 fusion.44
  856.1 9.1 collective-permute-done.1
  867.4 9.1 fusion.44
  931.2 9.1 fusion.44
  941.8 9.4 collective-permute-done.1
  963.9 10.4 collective-permute-done.1
  987.1 12.1 collective-permute-done.1
  1011.9 11.9 collective-permute-done.1
  1036.5 12.4 collective-permute-done.1
  1061.6 9.3 collective-permute-done.1
  1083.7 12.0 collective-permute-done.1
  1108.4 11.4 collective-permute-done.1
  1132.6 10.0 collective-permute-done.1
  1156.5 66.4 %all-to-all-start = ((bf16[32,24,768]{2,1,0:T(8,128)(2,1)}), bf16[32,24,768]{2,1,0:T(8,128)(2,1)S(1)}, u32[]{:S(2)}, u32[]{:S(2)}) async-start(bf16[32,24,768]{2,1,0:T(8,128)(2,1)} %bitcast.22), calls=%async_computation | async-start | bytes 2359296 | tf_op jit(solution)/shard_map/all_to_all | solution.py:129
  1223.9 28.2 %all-to-all-done = bf16[32,24,768]{2,1,0:T(8,128)(2,1)S(1)} async-done(((bf16[32,24,768]{2,1,0:T(8,128)(2,1)}), bf16[32,24,768]{2,1,0:T(8,128)(2,1)S(1)}, u32[]{:S(2)}, u32[]{:S(2)}) %all-to-all-start) | async-done | bytes 1179680 | tf_op jit(solution)/shard_map/all_to_all | solution.py:129
  (308 shorter events, 567.7 us)
Async XLA Ops:
  7.2 75.2 %all-gather.7.cloned.1.call-start = ((), (), s32[]{:S(2)}) async-start(), calls=%async_computation.2 | async-start | bytes 4866048 | tf_op jit(solution)/shard_map/all_gather | solution.py:62
  7.9 141.9 %all-gather.5.cloned.1.call-start = ((), (), s32[]{:S(2)}) async-start(), calls=%async_computation.1 | async-start | bytes 4866048 | tf_op jit(solution)/shard_map/all_gather | solution.py:63
  188.0 9.1 collective-permute-start
  208.4 10.1 collective-permute-start
  229.7 9.8 collective-permute-start
  250.7 10.1 collective-permute-start
  272.1 12.5 collective-permute-start
  295.7 11.2 collective-permute-start
  318.2 10.8 collective-permute-start
  340.2 10.7 collective-permute-start
  362.1 11.5 collective-permute-start
  384.8 11.5 collective-permute-start
  407.5 11.5 collective-permute-start
  430.2 11.5 collective-permute-start
  452.9 11.5 collective-permute-start
  475.6 11.8 collective-permute-start
  498.6 11.8 collective-permute-start
  521.6 11.9 collective-permute-start
  544.8 11.9 collective-permute-start
  567.9 12.5 collective-permute-start
  591.6 11.2 collective-permute-start
  614.0 11.4 collective-permute-start
  636.6 11.7 collective-permute-start
  648.6 493.9 %copy-start.1 = (f32[1,3072]{1,0:T(1,128)S(1)}, f32[1,3072]{1,0:T(1,128)}, u32[]{:S(2)}) copy-start(f32[1,3072]{1,0:T(1,128)} %param.12) | copy-start | bytes 36868
  660.0 11.5 collective-permute-start.1
  683.0 11.1 collective-permute-start.1
  705.5 14.5 %collective-permute-start.1 = (bf16[24,3072]{1,0:T(8,128)(2,1)S(1)}, bf16[24,3072]{1,0:T(8,128)(2,1)S(1)}, u32[]{:S(2)}, u32[]{:S(2)}) collective-permute-start(bf16[24,3072]{1,0:T(8,128)(2,1)S(1)} %fusion.45), channel_id=1, source_target_pairs={{32,0},{64,32},{96,64},{128,96},{160,128},{192,160},{224,192},{256... | collective-permute-start | bytes 442376 | tf_op jit(solution)/shard_map/while/body/eval_jaxpr/ppermute | solution.py:13
  731.4 11.8 collective-permute-start.1
  754.7 11.8 collective-permute-start.1
  777.8 12.7 %collective-permute-start.1 = (bf16[24,3072]{1,0:T(8,128)(2,1)S(1)}, bf16[24,3072]{1,0:T(8,128)(2,1)S(1)}, u32[]{:S(2)}, u32[]{:S(2)}) collective-permute-start(bf16[24,3072]{1,0:T(8,128)(2,1)S(1)} %fusion.45), channel_id=1, source_target_pairs={{32,0},{64,32},{96,64},{128,96},{160,128},{192,160},{224,192},{256... | collective-permute-start | bytes 442376 | tf_op jit(solution)/shard_map/while/body/eval_jaxpr/ppermute | solution.py:13
  802.0 15.5 %collective-permute-start.1 = (bf16[24,3072]{1,0:T(8,128)(2,1)S(1)}, bf16[24,3072]{1,0:T(8,128)(2,1)S(1)}, u32[]{:S(2)}, u32[]{:S(2)}) collective-permute-start(bf16[24,3072]{1,0:T(8,128)(2,1)S(1)} %fusion.45), channel_id=1, source_target_pairs={{32,0},{64,32},{96,64},{128,96},{160,128},{192,160},{224,192},{256... | collective-permute-start | bytes 442376 | tf_op jit(solution)/shard_map/while/body/eval_jaxpr/ppermute | solution.py:13
  828.9 14.5 %collective-permute-start.1 = (bf16[24,3072]{1,0:T(8,128)(2,1)S(1)}, bf16[24,3072]{1,0:T(8,128)(2,1)S(1)}, u32[]{:S(2)}, u32[]{:S(2)}) collective-permute-start(bf16[24,3072]{1,0:T(8,128)(2,1)S(1)} %fusion.45), channel_id=1, source_target_pairs={{32,0},{64,32},{96,64},{128,96},{160,128},{192,160},{224,192},{256... | collective-permute-start | bytes 442376 | tf_op jit(solution)/shard_map/while/body/eval_jaxpr/ppermute | solution.py:13
  854.8 10.4 collective-permute-start.1
  876.6 9.9 collective-permute-start.1
  897.9 9.8 collective-permute-start.1
  919.1 10.0 collective-permute-start.1
  940.5 10.7 collective-permute-start.1
  962.6 11.8 collective-permute-start.1
  985.7 13.4 %collective-permute-start.1 = (bf16[24,3072]{1,0:T(8,128)(2,1)S(1)}, bf16[24,3072]{1,0:T(8,128)(2,1)S(1)}, u32[]{:S(2)}, u32[]{:S(2)}) collective-permute-start(bf16[24,3072]{1,0:T(8,128)(2,1)S(1)} %fusion.45), channel_id=1, source_target_pairs={{32,0},{64,32},{96,64},{128,96},{160,128},{192,160},{224,192},{256... | collective-permute-start | bytes 442376 | tf_op jit(solution)/shard_map/while/body/eval_jaxpr/ppermute | solution.py:13
  1010.5 13.3 %collective-permute-start.1 = (bf16[24,3072]{1,0:T(8,128)(2,1)S(1)}, bf16[24,3072]{1,0:T(8,128)(2,1)S(1)}, u32[]{:S(2)}, u32[]{:S(2)}) collective-permute-start(bf16[24,3072]{1,0:T(8,128)(2,1)S(1)} %fusion.45), channel_id=1, source_target_pairs={{32,0},{64,32},{96,64},{128,96},{160,128},{192,160},{224,192},{256... | collective-permute-start | bytes 442376 | tf_op jit(solution)/shard_map/while/body/eval_jaxpr/ppermute | solution.py:13
  1035.2 13.7 %collective-permute-start.1 = (bf16[24,3072]{1,0:T(8,128)(2,1)S(1)}, bf16[24,3072]{1,0:T(8,128)(2,1)S(1)}, u32[]{:S(2)}, u32[]{:S(2)}) collective-permute-start(bf16[24,3072]{1,0:T(8,128)(2,1)S(1)} %fusion.45), channel_id=1, source_target_pairs={{32,0},{64,32},{96,64},{128,96},{160,128},{192,160},{224,192},{256... | collective-permute-start | bytes 442376 | tf_op jit(solution)/shard_map/while/body/eval_jaxpr/ppermute | solution.py:13
  1060.3 10.7 collective-permute-start.1
  1082.4 13.3 %collective-permute-start.1 = (bf16[24,3072]{1,0:T(8,128)(2,1)S(1)}, bf16[24,3072]{1,0:T(8,128)(2,1)S(1)}, u32[]{:S(2)}, u32[]{:S(2)}) collective-permute-start(bf16[24,3072]{1,0:T(8,128)(2,1)S(1)} %fusion.45), channel_id=1, source_target_pairs={{32,0},{64,32},{96,64},{128,96},{160,128},{192,160},{224,192},{256... | collective-permute-start | bytes 442376 | tf_op jit(solution)/shard_map/while/body/eval_jaxpr/ppermute | solution.py:13
  1107.0 12.8 %collective-permute-start.1 = (bf16[24,3072]{1,0:T(8,128)(2,1)S(1)}, bf16[24,3072]{1,0:T(8,128)(2,1)S(1)}, u32[]{:S(2)}, u32[]{:S(2)}) collective-permute-start(bf16[24,3072]{1,0:T(8,128)(2,1)S(1)} %fusion.45), channel_id=1, source_target_pairs={{32,0},{64,32},{96,64},{128,96},{160,128},{192,160},{224,192},{256... | collective-permute-start | bytes 442376 | tf_op jit(solution)/shard_map/while/body/eval_jaxpr/ppermute | solution.py:13
  1131.2 11.3 collective-permute-start.1
  1143.8 7.6 copy-start
  1156.5 95.6 %all-to-all-start = ((bf16[32,24,768]{2,1,0:T(8,128)(2,1)}), bf16[32,24,768]{2,1,0:T(8,128)(2,1)S(1)}, u32[]{:S(2)}, u32[]{:S(2)}) async-start(bf16[32,24,768]{2,1,0:T(8,128)(2,1)} %bitcast.22), calls=%async_computation | async-start | bytes 2359296 | tf_op jit(solution)/shard_map/all_to_all | solution.py:129
Sparse Core Ops, SparseCore 0:
  10.1 72.1 all-gather.6
  84.5 65.3 all-gather.4

commit v2 on v1

v2 whole, which is shorter than its diff:
```python
import functools

import jax
import jax.numpy as jnp
from jax import lax
from jax.experimental import pallas as pl
from jax.experimental.pallas import tpu as pltpu
from jax.sharding import PartitionSpec as P

epsilon = 1e-05


def whole_kernel(right_ref, rows_ref, owner_ref, gain_ref, whole_ref):
    column_block = pl.program_id(1)
    spread = jnp.where(
        owner_ref[...] == column_block, rows_ref[...].astype(jnp.float32), 0.0
    ).astype(jnp.bfloat16)
    product = jnp.dot(right_ref[...], spread, preferred_element_type=jnp.float32)
    whole_ref[...] = (product * gain_ref[...]).astype(jnp.bfloat16)


def build_maps(gain_row, order, right_full, left_full):
    channels, block = left_full.shape
    count = channels // block
    inverse = jnp.zeros((channels,), jnp.int32).at[order].set(jnp.arange(channels, dtype=jnp.int32))
    rows = jnp.take(left_full, inverse, axis=0)
    whole = pl.pallas_call(
        whole_kernel,
        grid=(count, count),
        in_specs=[
            pl.BlockSpec((block, block), lambda n, b: (n, 0)),
            pl.BlockSpec((block, block), lambda n, b: (n, 0)),
            pl.BlockSpec((block, 1), lambda n, b: (n, 0)),
            pl.BlockSpec((block, 1), lambda n, b: (n, 0)),
        ],
        out_specs=pl.BlockSpec((block, block), lambda n, b: (n, b)),
        out_shape=jax.ShapeDtypeStruct((channels, channels), jnp.bfloat16),
        name="whole_map",
    )(right_full, rows, (inverse // block)[:, None], gain_row[:, None])
    pick = (order[None, :block] == jnp.arange(channels)[:, None]).astype(jnp.bfloat16)
    head = jnp.einsum(
        "nkj,nji->nki",
        right_full.reshape(count, block, block),
        pick.reshape(count, block, block),
        preferred_element_type=jnp.float32,
    ).astype(jnp.bfloat16).reshape(channels, block)
    return whole, head


def inverse_norm(wide_in):
    return lax.rsqrt(jnp.mean(wide_in * wide_in, axis=-1, keepdims=True) + epsilon)


def relay_kernel(
    sections, in_ref, grad_ref, whole_ref, out_ref, saved_ref, up_ref,
    held, upstream, sent, scaled, forward_send, forward_recv, backward_send, backward_recv,
):
    me = lax.axis_index("section")
    micro_count, row_count, channels = held.shape
    chunk = up_ref.shape[2]
    after = lax.rem(me + 1, sections)
    ahead = lax.rem(me + sections - 1, sections)

    barrier = pltpu.get_barrier_semaphore()
    for neighbour in (after, ahead):
        pl.semaphore_signal(
            barrier, inc=1, device_id={"section": neighbour}, device_id_type=pl.DeviceIdType.MESH
        )

    @pl.when(me == 0)
    def first_inputs():
        held[...] = in_ref[...]

    @pl.when(me == sections - 1)
    def last_grads():
        upstream[...] = grad_ref[...]

    pl.semaphore_wait(barrier, 2)

    def forward_copy(slot):
        return pltpu.make_async_remote_copy(
            src_ref=out_ref.at[slot],
            dst_ref=held.at[slot],
            send_sem=forward_send.at[slot],
            recv_sem=forward_recv.at[slot],
            device_id={"section": after},
            device_id_type=pl.DeviceIdType.MESH,
        )

    def backward_copy(slot):
        return pltpu.make_async_remote_copy(
            src_ref=sent.at[slot],
            dst_ref=upstream.at[slot],
            send_sem=backward_send.at[slot],
            recv_sem=backward_recv.at[slot],
            device_id={"section": ahead},
            device_id_type=pl.DeviceIdType.MESH,
        )

    def run_forward(slot):
        @pl.when(me > 0)
        def arrived():
            forward_copy(slot).wait_recv()

        wide = held[slot].astype(jnp.float32)
        inverse_rms = inverse_norm(wide)

        def columns(part, carry):
            cols = pl.ds(pl.multiple_of(part * chunk, chunk), chunk)
            product = jnp.dot(held[slot], whole_ref[:, cols], preferred_element_type=jnp.float32)
            out_ref[slot, :, cols] = (
                held[slot, :, cols].astype(jnp.float32) + inverse_rms * product
            ).astype(jnp.bfloat16)
            return carry

        lax.fori_loop(0, channels // chunk, columns, 0)

        @pl.when(me < sections - 1)
        def pass_on():
            forward_copy(slot).start()

    def run_backward(slot):
        @pl.when(me < sections - 1)
        def arrived():
            backward_copy(slot).wait_recv()

        @pl.when(me > 0)
        def compute():
            def columns(part, carry):
                cols = pl.ds(pl.multiple_of(part * chunk, chunk), chunk)
                scaled[:, cols] = lax.dot_general(
                    upstream[slot], whole_ref[cols, :], (((1,), (1,)), ((), ())),
                    preferred_element_type=jnp.float32,
                )
                return carry

            lax.fori_loop(0, channels // chunk, columns, 0)
            wide = held[slot].astype(jnp.float32)
            inverse_rms = inverse_norm(wide)
            terms = scaled[...]
            along = jnp.mean(terms * wide, axis=-1, keepdims=True)
            cubed = inverse_rms * inverse_rms * inverse_rms
            sent[slot] = (
                upstream[slot].astype(jnp.float32) + inverse_rms * terms - wide * (cubed * along)
            ).astype(jnp.bfloat16)
            backward_copy(slot).start()

    def tick(step, carry):
        forward_slot = step - me
        backward_slot = step - (2 * sections - 1) + me

        @pl.when((forward_slot >= 0) & (forward_slot < micro_count))
        def forward_part():
            run_forward(forward_slot)

        @pl.when((backward_slot >= 0) & (backward_slot < micro_count))
        def backward_part():
            run_backward(backward_slot)

        return carry

    lax.fori_loop(0, 2 * sections - 1 + micro_count, tick, 0)
    saved_ref[...] = held[...]
    up_ref[...] = upstream[:, :, :chunk]

    @pl.when(me < sections - 1)
    def forward_sent():
        for slot in range(micro_count):
            forward_copy(slot).wait_send()

    @pl.when(me > 0)
    def backward_sent():
        for slot in range(micro_count):
            backward_copy(slot).wait_send()


def relay(sections, section_input, loss_grad, whole, block_size):
    shape = section_input.shape
    head_shape = shape[:2] + (block_size,)
    vmem = pl.BlockSpec(memory_space=pltpu.VMEM)
    sems = pltpu.SemaphoreType.DMA((shape[0],))
    return pl.pallas_call(
        functools.partial(relay_kernel, sections),
        out_shape=[
            jax.ShapeDtypeStruct(shape, jnp.bfloat16),
            jax.ShapeDtypeStruct(shape, jnp.bfloat16),
            jax.ShapeDtypeStruct(head_shape, jnp.bfloat16),
        ],
        in_specs=[vmem] * 3,
        out_specs=[vmem] * 3,
        scratch_shapes=[
            pltpu.VMEM(shape, jnp.bfloat16),
            pltpu.VMEM(shape, jnp.bfloat16),
            pltpu.VMEM(shape, jnp.bfloat16),
            pltpu.VMEM(shape[1:], jnp.float32),
            sems, sems, sems, sems,
        ],
        compiler_params=pltpu.CompilerParams(
            collective_id=0, has_side_effects=True, vmem_limit_bytes=48 * 1024 * 1024
        ),
        name="relay",
    )(section_input, loss_grad, whole)


def per_device(section_input, loss_grad, norm_gain, channel_order, right_factor, left_factor):
    sections = lax.axis_size("section")
    micro_count, row_count, channels = section_input.shape
    block_size = right_factor.shape[2]
    left_full = lax.all_gather(left_factor[0], "dp", axis=0, tiled=True)
    right_full = lax.all_gather(right_factor[0], "dp", axis=0, tiled=True)
    gain_row = norm_gain[0]
    whole, head = build_maps(gain_row, channel_order[0], right_full, left_full)
    outputs, saved_in, saved_up = relay(sections, section_input, loss_grad, whole, block_size)

    row_total = micro_count * row_count
    wide_in = saved_in.reshape(row_total, channels).astype(jnp.float32)
    normed = (wide_in * inverse_norm(wide_in) * gain_row).astype(jnp.bfloat16)
    permuted = jnp.dot(normed, head, preferred_element_type=jnp.float32).astype(jnp.bfloat16)
    left_shard = left_gradient(permuted, saved_up.reshape(row_total, block_size))
    return (outputs[None], left_shard[None])


def left_gradient(left_rows, right_rows):
    peers = lax.axis_size("dp")
    block_size = left_rows.shape[1]
    term = lax.dot_general(
        left_rows, right_rows, (((0,), (0,)), ((), ())), preferred_element_type=jnp.float32
    ).astype(jnp.bfloat16)
    parts = lax.all_to_all(
        term.reshape(peers, block_size // peers, block_size), "dp", split_axis=0, concat_axis=0
    )
    return jnp.sum(parts.astype(jnp.float32), axis=0)


def solution(mesh):
    in_specs = (
        P(None, "dp", None),
        P(None, "dp", None),
        P("section", None),
        P("section", None),
        P("section", "dp", None),
        P("section", "dp", None),
    )
    out_specs = (P("section", None, "dp", None), P("section", "dp", None))
    return jax.shard_map(
        per_device, mesh=mesh, in_specs=in_specs, out_specs=out_specs, check_vma=False
    )
```

time: 1270 us -> 723 us (0.57)
  Pallas kernels: 26.7 us -> 489 us
  matrix products: 390 us -> 11.1 us
  waiting for transfers between devices: 401 us -> 131 us
  starting transfers between devices: 285 us -> 35.2 us
  other arithmetic: 54.9 us -> 7.76 us
  loops' own time: 27.6 us -> 0 us
  local copies, waits for them, and re-layouts: 60.2 us -> 35.1 us
    pallas_call x0 -> x1, Pallas kernels: none -> 462 us  [relay(): pl.pallas_call(functools.partial(relay_kernel, sections), out_shape=[jax....]
    dot_general x42 -> x0, matrix products: 378 us -> none  [the longest x21 190 us: backward_step(): lax.dot_general(upstream, whole, (((1,), (1,)), ((), ())), preferred_elem...]
    ppermute x42 -> x0, waiting for transfers between devices: 271 us -> none  [shifted(): return lax.ppermute(array, axis, pairs)]
    ppermute x42 -> x0, starting transfers between devices: 218 us -> none  [shifted(): return lax.ppermute(array, axis, pairs)]
    all_to_all x1, starting transfers between devices: 66.4 us -> 35.1 us  [left_gradient(): lax.all_to_all(term.reshape(peers, block_size // peers, block_size), 'dp'...]
    another operation x2 -> x0, loops' own time: 27.6 us -> none  [the longest x1 14.9 us: per_device(): (_, saved_up), _ = lax.scan(backward_step, (empty_rows, empty_head), steps)]
    dynamic_slice x42 -> x0, local copies, waits for them, and re-layouts: 24.5 us -> none  [per_device(): lax.scan(forward_step, (empty_rows, empty_buf, empty_buf), steps)]
    dynamic_update_slice x21 -> x0, other arithmetic: 20 us -> none  [forward_step(): saved_in = lax.dynamic_update_index_in_dim(saved_in, inputs, write, 0)]
  transfers between devices with their start and end apart: 45 -> 3, of which waited for: 45 -> 3; matrix products, arithmetic and copies ran while one was open for 3% -> 6% of each run, Pallas kernels for 0% -> 0%
where the time goes in v2:
time: 723 us
  Pallas kernels  489 us (68%)
  waiting for transfers between devices  131 us (18%)
  starting transfers between devices  35.2 us (5%)
  local copies, waits for them, and re-layouts  35.1 us (5%)
  between operations  14.1 us (2%)
  matrix products  11.1 us (2%)
  other arithmetic  7.76 us (1%)
    pallas_call x1, Pallas kernels, relay(): pl.pallas_call(functools.partial(relay_kernel, sections), out_shape=[jax....  462 us
    all_gather x1, waiting for transfers between devices, per_device(): left_full = lax.all_gather(left_factor[0], 'dp', axis=0, tiled=True)  56.3 us
    all_gather x1, waiting for transfers between devices, per_device(): right_full = lax.all_gather(right_factor[0], 'dp', axis=0, tiled=True)  44.2 us
    all_to_all x1, starting transfers between devices, left_gradient(): lax.all_to_all(term.reshape(peers, block_size // peers, block_size), 'dp'...  35.1 us
    all_to_all x1, waiting for transfers between devices, left_gradient(): lax.all_to_all(term.reshape(peers, block_size // peers, block_size), 'dp'...  29.2 us
    pallas_call x1, Pallas kernels, build_maps(): pl.pallas_call(whole_kernel, grid=(count, count), in_specs=[pl.BlockSpec(...  26.8 us
    gather x1, local copies, waits for them, and re-layouts, build_maps(): rows = jnp.take(left_full, inverse, axis=0)  17.6 us
  transfers between devices with their start and end apart: 3, of which 3 were waited for; matrix products, arithmetic and copies ran while one was open for 6% of the time, Pallas kernels for 0%

profile of v2, /device:TPU:1, one launch (start us, length us, event | category | flops | bytes accessed | tf_op | source)
XLA Modules:
  0.0 722.9 jit_solution(7927861196545645667)
XLA Ops:
  7.2 0.0 all-gather.7.cloned.1.call-start
  7.2 0.7 all-gather.7.cloned.1.call-update
  7.9 0.0 all-gather.5.cloned.1.call-start
  7.9 0.7 all-gather.5.cloned.1.call-update
  8.6 0.7 compare_select_fusion
  9.4 11.8 %scatter_custom_fusion = s32[3072]{0:T(1024)S(1)} fusion(s32[3072]{0:T(1024)S(1)} %bitcast.32, s32[3072]{0:T(1024)S(1)} %iota.14, s32[]{:T(128)} %constant.18.clone.1), kind=kCustom, calls=%fused_computation.25 | custom fusion | bytes 12292 | tf_op jit(solution)/shard_map/scatter | solution.py:25
  21.2 1.7 copy.8.owner_ref
  22.9 2.4 copy.9.gain_ref
  25.3 0.7 slice_reduce_fusion
  26.0 56.3 %all-gather.7.cloned.1.call-done = bf16[1,3072,768]{2,1,0:T(8,128)(2,1)} async-done(((bf16[1,96,768]{2,1,0:T(8,128)(2,1)}), bf16[1,3072,768]{2,1,0:T(8,128)(2,1)}) %all-gather.7.cloned.1.call-update) | async-done | bytes 4718608 | tf_op jit(solution)/shard_map/all_gather | solution.py:209
  82.3 17.6 %gather_fusion = bf16[3072,768]{1,0:T(8,128)(2,1)} fusion(bf16[3072,768]{1,0:T(8,128)(2,1)} %bitcast.23, s32[3072]{0:T(1024)S(1)} %get-tuple-element.9), kind=kCustom, calls=%fused_computation | custom fusion | bytes 9449472 | tf_op jit(solution)/shard_map/jit(_take)/gather | solution.py:26
  99.9 5.7 broadcast_select_fusion.rows_ref
  105.6 44.2 %all-gather.5.cloned.1.call-done = bf16[1,3072,768]{2,1,0:T(8,128)(2,1)} async-done(((bf16[1,96,768]{2,1,0:T(8,128)(2,1)}), bf16[1,3072,768]{2,1,0:T(8,128)(2,1)}) %all-gather.5.cloned.1.call-update) | async-done | bytes 4718608 | tf_op jit(solution)/shard_map/all_gather | solution.py:210
  149.8 0.0 copy-start
  149.8 0.0 copy-start.1
  149.8 26.8 %whole_map.1.whole_ref = bf16[3072,3072]{1,0:T(8,128)(2,1)} custom-call(bf16[3072,768]{1,0:T(8,128)(2,1)} %bitcast.25, bf16[3072,768]{1,0:T(8,128)(2,1)} %broadcast_select_fusion.rows_ref, s32[3072,1]{1,0:T(8,128)} %copy.8.owner_ref, f32[3072,1]{1,0:T(8,128)} %copy.9.gain_ref), custom_call_target="tpu_custom_call" | custom-call | tf_op jit(solution)/shard_map/whole_map/pallas_call | solution.py:27
  176.6 0.0 copy-done
  176.6 0.0 copy-done.1
  176.6 0.0 copy-start.3
  176.6 0.0 copy-start.2
  176.6 461.7 %relay.1 = (bf16[6,24,3072]{2,1,0:T(8,128)(2,1)S(1)}, bf16[6,24,3072]{2,1,0:T(8,128)(2,1)S(1)}, bf16[6,24,768]{2,1,0:T(8,128)(2,1)S(1)}) custom-call(bf16[6,24,3072]{2,1,0:T(8,128)(2,1)S(1)} %copy-done, bf16[6,24,3072]{2,1,0:T(8,128)(2,1)S(1)} %copy-done.1, bf16[3072,3072]{1,0:T(8,128)(2,1)} %whole_map.1.whole_ref), custom_call_target="tpu_custom_call" | custom-call | tf_op jit(solution)/shard_map/relay/pallas_call | solution.py:182
  638.3 0.2 fusion.7
  638.6 0.0 copy-done.3
  638.6 0.3 fusion.9
  638.9 0.0 copy-done.2
  638.9 5.9 fusion.4
  644.8 5.2 convolution_convert_fusion
  650.0 35.1 %all-to-all-start = ((bf16[32,24,768]{2,1,0:T(8,128)(2,1)}), bf16[32,24,768]{2,1,0:T(8,128)(2,1)S(1)}, u32[]{:S(2)}, u32[]{:S(2)}) async-start(bf16[32,24,768]{2,1,0:T(8,128)(2,1)} %bitcast.13), calls=%async_computation | async-start | bytes 2359296 | tf_op jit(solution)/shard_map/all_to_all | solution.py:229
  685.1 29.2 %all-to-all-done = bf16[32,24,768]{2,1,0:T(8,128)(2,1)S(1)} async-done(((bf16[32,24,768]{2,1,0:T(8,128)(2,1)}), bf16[32,24,768]{2,1,0:T(8,128)(2,1)S(1)}, u32[]{:S(2)}, u32[]{:S(2)}) %all-to-all-start) | async-done | bytes 1179680 | tf_op jit(solution)/shard_map/all_to_all | solution.py:229
  714.3 0.8 convert_reduce_fusion
  715.1 0.9 copy.11
  (5 shorter events, 0.0 us)
Async XLA Ops:
  7.2 75.2 %all-gather.7.cloned.1.call-start = ((), (), s32[]{:S(2)}) async-start(), calls=%async_computation.2 | async-start | bytes 4866048 | tf_op jit(solution)/shard_map/all_gather | solution.py:209
  7.9 141.9 %all-gather.5.cloned.1.call-start = ((), (), s32[]{:S(2)}) async-start(), calls=%async_computation.1 | async-start | bytes 4866048 | tf_op jit(solution)/shard_map/all_gather | solution.py:210
  149.8 26.8 %copy-start = (bf16[6,24,3072]{2,1,0:T(8,128)(2,1)S(1)}, bf16[6,24,3072]{2,1,0:T(8,128)(2,1)}, u32[]{:S(2)}) copy-start(bf16[6,24,3072]{2,1,0:T(8,128)(2,1)} %in_ref.1) | copy-start | bytes 2654212
  149.8 26.8 %copy-start.1 = (bf16[6,24,3072]{2,1,0:T(8,128)(2,1)S(1)}, bf16[6,24,3072]{2,1,0:T(8,128)(2,1)}, u32[]{:S(2)}) copy-start(bf16[6,24,3072]{2,1,0:T(8,128)(2,1)} %grad_ref.1) | copy-start | bytes 2654212
  176.6 462.0 %copy-start.3 = (f32[1,3072]{1,0:T(1,128)S(1)}, f32[1,3072]{1,0:T(1,128)}, u32[]{:S(2)}) copy-start(f32[1,3072]{1,0:T(1,128)} %param.8) | copy-start | bytes 36868
  176.6 462.3 %copy-start.2 = (bf16[1,3072,768]{2,1,0:T(8,128)(2,1)S(1)}, bf16[1,3072,768]{2,1,0:T(8,128)(2,1)}, u32[]{:S(2)}) copy-start(bf16[1,3072,768]{2,1,0:T(8,128)(2,1)} %all-gather.5.cloned.1.call-done) | copy-start | bytes 14155780
  650.0 64.3 %all-to-all-start = ((bf16[32,24,768]{2,1,0:T(8,128)(2,1)}), bf16[32,24,768]{2,1,0:T(8,128)(2,1)S(1)}, u32[]{:S(2)}, u32[]{:S(2)}) async-start(bf16[32,24,768]{2,1,0:T(8,128)(2,1)} %bitcast.13), calls=%async_computation | async-start | bytes 2359296 | tf_op jit(solution)/shard_map/all_to_all | solution.py:229
Sparse Core Ops, SparseCore 0:
  10.1 72.1 all-gather.6
  84.5 65.2 all-gather.4

commit v3 on v2

--- a/solution.py
+++ b/solution.py
@@ -8,6 +8,8 @@
 from jax.sharding import PartitionSpec as P
 
 epsilon = 1e-05
+piece_rows = 8
+ticks_per_hop = 2
 
 
 def whole_kernel(right_ref, rows_ref, owner_ref, gain_ref, whole_ref):
@@ -146,8 +148,8 @@
             backward_copy(slot).start()
 
     def tick(step, carry):
-        forward_slot = step - me
-        backward_slot = step - (2 * sections - 1) + me
+        forward_slot = step - ticks_per_hop * me
+        backward_slot = step - ticks_per_hop * (2 * sections - 2 - me) - 1
 
         @pl.when((forward_slot >= 0) & (forward_slot < micro_count))
         def forward_part():
@@ -159,19 +161,17 @@
 
         return carry
 
-    lax.fori_loop(0, 2 * sections - 1 + micro_count, tick, 0)
+    lax.fori_loop(0, ticks_per_hop * (2 * sections - 2) + 1 + micro_count, tick, 0)
     saved_ref[...] = held[...]
     up_ref[...] = upstream[:, :, :chunk]
 
     @pl.when(me < sections - 1)
     def forward_sent():
-        for slot in range(micro_count):
-            forward_copy(slot).wait_send()
+        lax.fori_loop(0, micro_count, lambda slot, carry: (forward_copy(slot).wait_send(), carry)[1], 0)
 
     @pl.when(me > 0)
     def backward_sent():
-        for slot in range(micro_count):
-            backward_copy(slot).wait_send()
+        lax.fori_loop(0, micro_count, lambda slot, carry: (backward_copy(slot).wait_send(), carry)[1], 0)
 
 
 def relay(sections, section_input, loss_grad, whole, block_size):
@@ -210,14 +210,17 @@
     right_full = lax.all_gather(right_factor[0], "dp", axis=0, tiled=True)
     gain_row = norm_gain[0]
     whole, head = build_maps(gain_row, channel_order[0], right_full, left_full)
-    outputs, saved_in, saved_up = relay(sections, section_input, loss_grad, whole, block_size)
+    pieces = (micro_count * row_count // piece_rows, piece_rows, channels)
+    outputs, saved_in, saved_up = relay(
+        sections, section_input.reshape(pieces), loss_grad.reshape(pieces), whole, block_size
+    )
 
     row_total = micro_count * row_count
     wide_in = saved_in.reshape(row_total, channels).astype(jnp.float32)
     normed = (wide_in * inverse_norm(wide_in) * gain_row).astype(jnp.bfloat16)
     permuted = jnp.dot(normed, head, preferred_element_type=jnp.float32).astype(jnp.bfloat16)
     left_shard = left_gradient(permuted, saved_up.reshape(row_total, block_size))
-    return (outputs[None], left_shard[None])
+    return (outputs.reshape(section_input.shape)[None], left_shard[None])
 
 
 def left_gradient(left_rows, right_rows):

time: 723 us -> 691 us (0.956)
  Pallas kernels: 489 us -> 455 us
    pallas_call x1, Pallas kernels: 462 us -> 429 us  [relay(): pl.pallas_call(functools.partial(relay_kernel, sections), out_shape=[jax....]
where the time goes in v3:
time: 691 us; the launch traced here: 690 us
  Pallas kernels  455 us (66%)
  waiting for transfers between devices  131 us (19%)
  starting transfers between devices  36 us (5%)
  local copies, waits for them, and re-layouts  35.2 us (5%)
  between operations  14.1 us (2%)
  matrix products  11.2 us (2%)
  other arithmetic  7.46 us (1%)
    pallas_call x1, Pallas kernels, relay(): pl.pallas_call(functools.partial(relay_kernel, sections), out_shape=[jax....  429 us
    all_gather x1, waiting for transfers between devices, per_device(): left_full = lax.all_gather(left_factor[0], 'dp', axis=0, tiled=True)  56.3 us
    all_gather x1, waiting for transfers between devices, per_device(): right_full = lax.all_gather(right_factor[0], 'dp', axis=0, tiled=True)  44.1 us
    all_to_all x1, starting transfers between devices, left_gradient(): lax.all_to_all(term.reshape(peers, block_size // peers, block_size), 'dp'...  36 us
    all_to_all x1, waiting for transfers between devices, left_gradient(): lax.all_to_all(term.reshape(peers, block_size // peers, block_size), 'dp'...  29.2 us
    pallas_call x1, Pallas kernels, build_maps(): pl.pallas_call(whole_kernel, grid=(count, count), in_specs=[pl.BlockSpec(...  26.9 us
    gather x1, local copies, waits for them, and re-layouts, build_maps(): rows = jnp.take(left_full, inverse, axis=0)  17.7 us
  transfers between devices with their start and end apart: 3, of which 3 were waited for; matrix products, arithmetic and copies ran while one was open for 6% of the time, Pallas kernels for 0%

profile of v3, /device:TPU:1, one launch (start us, length us, event | category | flops | bytes accessed | tf_op | source)
XLA Modules:
  0.0 690.4 jit_solution(1084206269040440352)
XLA Ops:
  7.2 0.0 all-gather.7.cloned.1.call-start
  7.2 0.7 all-gather.7.cloned.1.call-update
  7.9 0.0 all-gather.5.cloned.1.call-start
  7.9 0.7 all-gather.5.cloned.1.call-update
  8.6 0.7 compare_select_fusion
  9.4 11.8 %scatter_custom_fusion = s32[3072]{0:T(1024)S(1)} fusion(s32[3072]{0:T(1024)S(1)} %bitcast.36, s32[3072]{0:T(1024)S(1)} %iota.14, s32[]{:T(128)} %constant.18.clone.1), kind=kCustom, calls=%fused_computation.30 | custom fusion | bytes 12292 | tf_op jit(solution)/shard_map/scatter | solution.py:27
  21.2 1.7 copy.8.owner_ref
  22.9 2.4 copy.9.gain_ref
  25.3 0.7 slice_reduce_fusion
  26.0 56.3 %all-gather.7.cloned.1.call-done = bf16[1,3072,768]{2,1,0:T(8,128)(2,1)} async-done(((bf16[1,96,768]{2,1,0:T(8,128)(2,1)}), bf16[1,3072,768]{2,1,0:T(8,128)(2,1)}) %all-gather.7.cloned.1.call-update) | async-done | bytes 4718608 | tf_op jit(solution)/shard_map/all_gather | solution.py:209
  82.3 17.7 %gather_fusion = bf16[3072,768]{1,0:T(8,128)(2,1)} fusion(bf16[3072,768]{1,0:T(8,128)(2,1)} %bitcast.29, s32[3072]{0:T(1024)S(1)} %get-tuple-element.9), kind=kCustom, calls=%fused_computation | custom fusion | bytes 9449472 | tf_op jit(solution)/shard_map/jit(_take)/gather | solution.py:28
  100.0 5.6 broadcast_select_fusion.rows_ref
  105.6 44.1 %all-gather.5.cloned.1.call-done = bf16[1,3072,768]{2,1,0:T(8,128)(2,1)} async-done(((bf16[1,96,768]{2,1,0:T(8,128)(2,1)}), bf16[1,3072,768]{2,1,0:T(8,128)(2,1)}) %all-gather.5.cloned.1.call-update) | async-done | bytes 4718608 | tf_op jit(solution)/shard_map/all_gather | solution.py:210
  149.8 0.0 copy-start
  149.8 0.0 copy-start.1
  149.8 26.9 %whole_map.1.whole_ref = bf16[3072,3072]{1,0:T(8,128)(2,1)} custom-call(bf16[3072,768]{1,0:T(8,128)(2,1)} %bitcast.30, bf16[3072,768]{1,0:T(8,128)(2,1)} %broadcast_select_fusion.rows_ref, s32[3072,1]{1,0:T(8,128)} %copy.8.owner_ref, f32[3072,1]{1,0:T(8,128)} %copy.9.gain_ref), custom_call_target="tpu_custom_call" | custom-call | tf_op jit(solution)/shard_map/whole_map/pallas_call | solution.py:29
  176.6 0.0 copy-done
  176.6 0.0 copy-done.1
  176.6 0.0 copy-start.3
  176.7 428.6 %relay.1 = (bf16[18,8,3072]{2,1,0:T(8,128)(2,1)S(1)}, bf16[18,8,3072]{2,1,0:T(8,128)(2,1)S(1)}, bf16[18,8,768]{2,1,0:T(8,128)(2,1)S(1)}) custom-call(bf16[18,8,3072]{2,1,0:T(8,128)(2,1)S(1)} %bitcast.27, bf16[18,8,3072]{2,1,0:T(8,128)(2,1)S(1)} %bitcast.28, bf16[3072,3072]{1,0:T(8,128)(2,1)} %whole_map.1.whole_ref), custom_call_target="tpu_custom_call" | custom-call | tf_op jit(solution)/shard_map/relay/pallas_call | solution.py:182
  605.2 0.0 copy-start.2
  605.2 0.3 fusion.7
  605.5 0.0 copy-done.3
  605.5 0.0 copy-start.4
  605.5 5.9 fusion.4
  611.5 0.0 copy-done.2
  611.5 0.0 copy-done.4
  611.5 5.2 convolution_convert_fusion
  616.7 36.0 %all-to-all-start = ((bf16[32,24,768]{2,1,0:T(8,128)(2,1)}), bf16[32,24,768]{2,1,0:T(8,128)(2,1)S(1)}, u32[]{:S(2)}, u32[]{:S(2)}) async-start(bf16[32,24,768]{2,1,0:T(8,128)(2,1)} %bitcast.15), calls=%async_computation | async-start | bytes 2359296 | tf_op jit(solution)/shard_map/all_to_all | solution.py:232
  652.7 29.2 %all-to-all-done = bf16[32,24,768]{2,1,0:T(8,128)(2,1)S(1)} async-done(((bf16[32,24,768]{2,1,0:T(8,128)(2,1)}), bf16[32,24,768]{2,1,0:T(8,128)(2,1)S(1)}, u32[]{:S(2)}, u32[]{:S(2)}) %all-to-all-start) | async-done | bytes 1179680 | tf_op jit(solution)/shard_map/all_to_all | solution.py:232
  681.9 0.8 convert_reduce_fusion
  682.7 0.9 copy.11
  (5 shorter events, 0.0 us)
Async XLA Ops:
  7.2 75.2 %all-gather.7.cloned.1.call-start = ((), (), s32[]{:S(2)}) async-start(), calls=%async_computation.2 | async-start | bytes 4866048 | tf_op jit(solution)/shard_map/all_gather | solution.py:209
  7.9 141.9 %all-gather.5.cloned.1.call-start = ((), (), s32[]{:S(2)}) async-start(), calls=%async_computation.1 | async-start | bytes 4866048 | tf_op jit(solution)/shard_map/all_gather | solution.py:210
  149.8 26.9 %copy-start = (bf16[6,24,3072]{2,1,0:T(8,128)(2,1)S(1)}, bf16[6,24,3072]{2,1,0:T(8,128)(2,1)}, u32[]{:S(2)}) copy-start(bf16[6,24,3072]{2,1,0:T(8,128)(2,1)} %param.6) | copy-start | bytes 2654212
  149.8 26.9 %copy-start.1 = (bf16[6,24,3072]{2,1,0:T(8,128)(2,1)S(1)}, bf16[6,24,3072]{2,1,0:T(8,128)(2,1)}, u32[]{:S(2)}) copy-start(bf16[6,24,3072]{2,1,0:T(8,128)(2,1)} %param.7) | copy-start | bytes 2654212
  176.6 428.9 %copy-start.3 = (bf16[1,3072,768]{2,1,0:T(8,128)(2,1)S(1)}, bf16[1,3072,768]{2,1,0:T(8,128)(2,1)}, u32[]{:S(2)}) copy-start(bf16[1,3072,768]{2,1,0:T(8,128)(2,1)} %all-gather.5.cloned.1.call-done) | copy-start | bytes 14155780
  605.2 6.2 copy-start.2
  605.5 6.0 copy-start.4
  616.7 65.2 %all-to-all-start = ((bf16[32,24,768]{2,1,0:T(8,128)(2,1)}), bf16[32,24,768]{2,1,0:T(8,128)(2,1)S(1)}, u32[]{:S(2)}, u32[]{:S(2)}) async-start(bf16[32,24,768]{2,1,0:T(8,128)(2,1)} %bitcast.15), calls=%async_computation | async-start | bytes 2359296 | tf_op jit(solution)/shard_map/all_to_all | solution.py:232
Sparse Core Ops, SparseCore 0:
  10.1 72.1 all-gather.6
  84.5 65.2 all-gather.4

commit v4 on v3

--- a/solution.py
+++ b/solution.py
@@ -8,7 +8,7 @@
 from jax.sharding import PartitionSpec as P
 
 epsilon = 1e-05
-piece_rows = 8
+piece_rows = 16
 ticks_per_hop = 2
 
 
@@ -79,12 +79,15 @@
 
     pl.semaphore_wait(barrier, 2)
 
-    def forward_copy(slot):
+    parts = channels // chunk
+
+    def forward_copy(slot, part):
+        cols = pl.ds(pl.multiple_of(part * chunk, chunk), chunk)
         return pltpu.make_async_remote_copy(
-            src_ref=out_ref.at[slot],
-            dst_ref=held.at[slot],
-            send_sem=forward_send.at[slot],
-            recv_sem=forward_recv.at[slot],
+            src_ref=out_ref.at[slot, :, cols],
+            dst_ref=held.at[slot, :, cols],
+            send_sem=forward_send.at[slot, part],
+            recv_sem=forward_recv.at[slot, part],
             device_id={"section": after},
             device_id_type=pl.DeviceIdType.MESH,
         )
@@ -102,7 +105,8 @@
     def run_forward(slot):
         @pl.when(me > 0)
         def arrived():
-            forward_copy(slot).wait_recv()
+            for part in range(parts):
+                forward_copy(slot, part).wait_recv()
 
         wide = held[slot].astype(jnp.float32)
         inverse_rms = inverse_norm(wide)
@@ -113,13 +117,14 @@
             out_ref[slot, :, cols] = (
                 held[slot, :, cols].astype(jnp.float32) + inverse_rms * product
             ).astype(jnp.bfloat16)
+
+            @pl.when(me < sections - 1)
+            def pass_on():
+                forward_copy(slot, part).start()
+
             return carry
 
-        lax.fori_loop(0, channels // chunk, columns, 0)
-
-        @pl.when(me < sections - 1)
-        def pass_on():
-            forward_copy(slot).start()
+        lax.fori_loop(0, parts, columns, 0)
 
     def run_backward(slot):
         @pl.when(me < sections - 1)
@@ -136,7 +141,7 @@
                 )
                 return carry
 
-            lax.fori_loop(0, channels // chunk, columns, 0)
+            lax.fori_loop(0, parts, columns, 0)
             wide = held[slot].astype(jnp.float32)
             inverse_rms = inverse_norm(wide)
             terms = scaled[...]
@@ -167,7 +172,12 @@
 
     @pl.when(me < sections - 1)
     def forward_sent():
-        lax.fori_loop(0, micro_count, lambda slot, carry: (forward_copy(slot).wait_send(), carry)[1], 0)
+        def sent_piece(slot, carry):
+            for part in range(parts):
+                forward_copy(slot, part).wait_send()
+            return carry
+
+        lax.fori_loop(0, micro_count, sent_piece, 0)
 
     @pl.when(me > 0)
     def backward_sent():
@@ -179,6 +189,7 @@
     head_shape = shape[:2] + (block_size,)
     vmem = pl.BlockSpec(memory_space=pltpu.VMEM)
     sems = pltpu.SemaphoreType.DMA((shape[0],))
+    part_sems = pltpu.SemaphoreType.DMA((shape[0], shape[2] // block_size))
     return pl.pallas_call(
         functools.partial(relay_kernel, sections),
         out_shape=[
@@ -193,7 +204,7 @@
             pltpu.VMEM(shape, jnp.bfloat16),
             pltpu.VMEM(shape, jnp.bfloat16),
             pltpu.VMEM(shape[1:], jnp.float32),
-            sems, sems, sems, sems,
+            part_sems, part_sems, sems, sems,
         ],
         compiler_params=pltpu.CompilerParams(
             collective_id=0, has_side_effects=True, vmem_limit_bytes=48 * 1024 * 1024

time: 691 us -> 643 us (0.931)
  Pallas kernels: 455 us -> 401 us
    pallas_call x1, Pallas kernels: 429 us -> 375 us  [relay(): pl.pallas_call(functools.partial(relay_kernel, sections), out_shape=[jax....]
where the time goes in v4:
time: 643 us; the launch traced here: 642 us
  Pallas kernels  401 us (62%)
  waiting for transfers between devices  131 us (20%)
  starting transfers between devices  41.6 us (6%)
  local copies, waits for them, and re-layouts  35.1 us (5%)
  between operations  14.1 us (2%)
  matrix products  11.1 us (2%)
  other arithmetic  7.73 us (1%)
    pallas_call x1, Pallas kernels, relay(): pl.pallas_call(functools.partial(relay_kernel, sections), out_shape=[jax....  375 us
    all_gather x1, waiting for transfers between devices, per_device(): left_full = lax.all_gather(left_factor[0], 'dp', axis=0, tiled=True)  56.3 us
    all_gather x1, waiting for transfers between devices, per_device(): right_full = lax.all_gather(right_factor[0], 'dp', axis=0, tiled=True)  44.2 us
    all_to_all x1, starting transfers between devices, left_gradient(): lax.all_to_all(term.reshape(peers, block_size // peers, block_size), 'dp'...  41.5 us
    all_to_all x1, waiting for transfers between devices, left_gradient(): lax.all_to_all(term.reshape(peers, block_size // peers, block_size), 'dp'...  29.2 us
    pallas_call x1, Pallas kernels, build_maps(): pl.pallas_call(whole_kernel, grid=(count, count), in_specs=[pl.BlockSpec(...  26.8 us
    gather x1, local copies, waits for them, and re-layouts, build_maps(): rows = jnp.take(left_full, inverse, axis=0)  17.6 us
  transfers between devices with their start and end apart: 3, of which 3 were waited for; matrix products, arithmetic and copies ran while one was open for 6% of the time, Pallas kernels for 0%

profile of v4, /device:TPU:1, one launch (start us, length us, event | category | flops | bytes accessed | tf_op | source)
XLA Modules:
  0.0 642.2 jit_solution(11896532501340586148)
XLA Ops:
  7.2 0.0 all-gather.7.cloned.1.call-start
  7.2 0.7 all-gather.7.cloned.1.call-update
  7.9 0.0 all-gather.5.cloned.1.call-start
  7.9 0.7 all-gather.5.cloned.1.call-update
  8.6 0.7 compare_select_fusion
  9.4 11.8 %scatter_custom_fusion = s32[3072]{0:T(1024)S(1)} fusion(s32[3072]{0:T(1024)S(1)} %bitcast.36, s32[3072]{0:T(1024)S(1)} %iota.14, s32[]{:T(128)} %constant.18.clone.1), kind=kCustom, calls=%fused_computation.26 | custom fusion | bytes 12292 | tf_op jit(solution)/shard_map/scatter | solution.py:27
  21.2 1.7 copy.8.owner_ref
  22.9 2.4 copy.9.gain_ref
  25.3 0.7 slice_reduce_fusion
  26.0 56.3 %all-gather.7.cloned.1.call-done = bf16[1,3072,768]{2,1,0:T(8,128)(2,1)} async-done(((bf16[1,96,768]{2,1,0:T(8,128)(2,1)}), bf16[1,3072,768]{2,1,0:T(8,128)(2,1)}) %all-gather.7.cloned.1.call-update) | async-done | bytes 4718608 | tf_op jit(solution)/shard_map/all_gather | solution.py:220
  82.3 17.6 %gather_fusion = bf16[3072,768]{1,0:T(8,128)(2,1)} fusion(bf16[3072,768]{1,0:T(8,128)(2,1)} %bitcast.27, s32[3072]{0:T(1024)S(1)} %get-tuple-element.9), kind=kCustom, calls=%fused_computation | custom fusion | bytes 9449472 | tf_op jit(solution)/shard_map/jit(_take)/gather | solution.py:28
  99.9 5.7 broadcast_select_fusion.rows_ref
  105.6 44.2 %all-gather.5.cloned.1.call-done = bf16[1,3072,768]{2,1,0:T(8,128)(2,1)} async-done(((bf16[1,96,768]{2,1,0:T(8,128)(2,1)}), bf16[1,3072,768]{2,1,0:T(8,128)(2,1)}) %all-gather.5.cloned.1.call-update) | async-done | bytes 4718608 | tf_op jit(solution)/shard_map/all_gather | solution.py:221
  149.8 0.0 copy-start
  149.8 0.0 copy-start.1
  149.8 26.8 %whole_map.1.whole_ref = bf16[3072,3072]{1,0:T(8,128)(2,1)} custom-call(bf16[3072,768]{1,0:T(8,128)(2,1)} %bitcast.29, bf16[3072,768]{1,0:T(8,128)(2,1)} %broadcast_select_fusion.rows_ref, s32[3072,1]{1,0:T(8,128)} %copy.8.owner_ref, f32[3072,1]{1,0:T(8,128)} %copy.9.gain_ref), custom_call_target="tpu_custom_call" | custom-call | tf_op jit(solution)/shard_map/whole_map/pallas_call | solution.py:29
  176.6 0.0 copy-done
  176.6 0.0 copy-done.1
  176.6 0.0 copy-start.3
  176.6 0.0 copy-start.2
  176.6 374.6 %relay.1 = (bf16[9,16,3072]{2,1,0:T(8,128)(2,1)S(1)}, bf16[9,16,3072]{2,1,0:T(8,128)(2,1)S(1)}, bf16[9,16,768]{2,1,0:T(8,128)(2,1)S(1)}) custom-call(bf16[9,16,3072]{2,1,0:T(8,128)(2,1)S(1)} %bitcast.24, bf16[9,16,3072]{2,1,0:T(8,128)(2,1)S(1)} %bitcast.25, bf16[3072,3072]{1,0:T(8,128)(2,1)} %whole_map.1.whole_ref), custom_call_target="tpu_custom_call" | custom-call | tf_op jit(solution)/shard_map/relay/pallas_call | solution.py:193
  551.3 0.2 fusion.7
  551.5 0.0 copy-done.3
  551.6 0.3 fusion.9
  551.8 0.0 copy-done.2
  551.9 5.9 fusion.4
  557.8 5.2 convolution_convert_fusion
  562.9 41.5 %all-to-all-start = ((bf16[32,24,768]{2,1,0:T(8,128)(2,1)}), bf16[32,24,768]{2,1,0:T(8,128)(2,1)S(1)}, u32[]{:S(2)}, u32[]{:S(2)}) async-start(bf16[32,24,768]{2,1,0:T(8,128)(2,1)} %bitcast.15), calls=%async_computation | async-start | bytes 2359296 | tf_op jit(solution)/shard_map/all_to_all | solution.py:243
  604.5 29.2 %all-to-all-done = bf16[32,24,768]{2,1,0:T(8,128)(2,1)S(1)} async-done(((bf16[32,24,768]{2,1,0:T(8,128)(2,1)}), bf16[32,24,768]{2,1,0:T(8,128)(2,1)S(1)}, u32[]{:S(2)}, u32[]{:S(2)}) %all-to-all-start) | async-done | bytes 1179680 | tf_op jit(solution)/shard_map/all_to_all | solution.py:243
  633.7 0.8 convert_reduce_fusion
  634.5 0.9 copy.11
  (5 shorter events, 0.0 us)
Async XLA Ops:
  7.2 75.2 %all-gather.7.cloned.1.call-start = ((), (), s32[]{:S(2)}) async-start(), calls=%async_computation.2 | async-start | bytes 4866048 | tf_op jit(solution)/shard_map/all_gather | solution.py:220
  7.9 141.9 %all-gather.5.cloned.1.call-start = ((), (), s32[]{:S(2)}) async-start(), calls=%async_computation.1 | async-start | bytes 4866048 | tf_op jit(solution)/shard_map/all_gather | solution.py:221
  149.8 26.8 %copy-start = (bf16[6,24,3072]{2,1,0:T(8,128)(2,1)S(1)}, bf16[6,24,3072]{2,1,0:T(8,128)(2,1)}, u32[]{:S(2)}) copy-start(bf16[6,24,3072]{2,1,0:T(8,128)(2,1)} %param.6) | copy-start | bytes 2654212
  149.8 26.8 %copy-start.1 = (bf16[6,24,3072]{2,1,0:T(8,128)(2,1)S(1)}, bf16[6,24,3072]{2,1,0:T(8,128)(2,1)}, u32[]{:S(2)}) copy-start(bf16[6,24,3072]{2,1,0:T(8,128)(2,1)} %param.7) | copy-start | bytes 2654212
  176.6 374.9 %copy-start.3 = (f32[1,3072]{1,0:T(1,128)S(1)}, f32[1,3072]{1,0:T(1,128)}, u32[]{:S(2)}) copy-start(f32[1,3072]{1,0:T(1,128)} %param.8) | copy-start | bytes 36868
  176.6 375.2 %copy-start.2 = (bf16[1,3072,768]{2,1,0:T(8,128)(2,1)S(1)}, bf16[1,3072,768]{2,1,0:T(8,128)(2,1)}, u32[]{:S(2)}) copy-start(bf16[1,3072,768]{2,1,0:T(8,128)(2,1)} %all-gather.5.cloned.1.call-done) | copy-start | bytes 14155780
  562.9 70.7 %all-to-all-start = ((bf16[32,24,768]{2,1,0:T(8,128)(2,1)}), bf16[32,24,768]{2,1,0:T(8,128)(2,1)S(1)}, u32[]{:S(2)}, u32[]{:S(2)}) async-start(bf16[32,24,768]{2,1,0:T(8,128)(2,1)} %bitcast.15), calls=%async_computation | async-start | bytes 2359296 | tf_op jit(solution)/shard_map/all_to_all | solution.py:243
Sparse Core Ops, SparseCore 0:
  10.1 72.1 all-gather.6
  84.5 65.2 all-gather.4

commit v5 on v4

--- a/solution.py
+++ b/solution.py
@@ -126,31 +126,41 @@
 
         lax.fori_loop(0, parts, columns, 0)
 
+    def back_product(slot):
+        def columns(part, carry):
+            cols = pl.ds(pl.multiple_of(part * chunk, chunk), chunk)
+            scaled[slot, :, cols] = lax.dot_general(
+                upstream[slot], whole_ref[cols, :], (((1,), (1,)), ((), ())),
+                preferred_element_type=jnp.float32,
+            )
+            return carry
+
+        lax.fori_loop(0, parts, columns, 0)
+
     def run_backward(slot):
         @pl.when(me < sections - 1)
         def arrived():
             backward_copy(slot).wait_recv()
 
+        @pl.when((me > 0) & (me < sections - 1))
+        def product():
+            back_product(slot)
+
         @pl.when(me > 0)
         def compute():
-            def columns(part, carry):
-                cols = pl.ds(pl.multiple_of(part * chunk, chunk), chunk)
-                scaled[:, cols] = lax.dot_general(
-                    upstream[slot], whole_ref[cols, :], (((1,), (1,)), ((), ())),
-                    preferred_element_type=jnp.float32,
-                )
-                return carry
-
-            lax.fori_loop(0, parts, columns, 0)
             wide = held[slot].astype(jnp.float32)
             inverse_rms = inverse_norm(wide)
-            terms = scaled[...]
+            terms = scaled[slot]
             along = jnp.mean(terms * wide, axis=-1, keepdims=True)
             cubed = inverse_rms * inverse_rms * inverse_rms
             sent[slot] = (
                 upstream[slot].astype(jnp.float32) + inverse_rms * terms - wide * (cubed * along)
             ).astype(jnp.bfloat16)
             backward_copy(slot).start()
+
+    @pl.when(me == sections - 1)
+    def products_ahead():
+        lax.fori_loop(0, micro_count, lambda slot, carry: (back_product(slot), carry)[1], 0)
 
     def tick(step, carry):
         forward_slot = step - ticks_per_hop * me
@@ -203,7 +213,7 @@
             pltpu.VMEM(shape, jnp.bfloat16),
             pltpu.VMEM(shape, jnp.bfloat16),
             pltpu.VMEM(shape, jnp.bfloat16),
-            pltpu.VMEM(shape[1:], jnp.float32),
+            pltpu.VMEM(shape, jnp.float32),
             part_sems, part_sems, sems, sems,
         ],
         compiler_params=pltpu.CompilerParams(

time: 643 us -> 638 us (level)
  no operation moved by 1% of the time
where the time goes in v5:
time: 638 us
  Pallas kernels  399 us (63%)
  waiting for transfers between devices  131 us (21%)
  starting transfers between devices  39.8 us (6%)
  local copies, waits for them, and re-layouts  35.1 us (6%)
  between operations  14.1 us (2%)
  matrix products  11.1 us (2%)
  other arithmetic  7.73 us (1%)
    pallas_call x1, Pallas kernels, relay(): pl.pallas_call(functools.partial(relay_kernel, sections), out_shape=[jax....  372 us
    all_gather x1, waiting for transfers between devices, per_device(): left_full = lax.all_gather(left_factor[0], 'dp', axis=0, tiled=True)  56.3 us
    all_gather x1, waiting for transfers between devices, per_device(): right_full = lax.all_gather(right_factor[0], 'dp', axis=0, tiled=True)  44.2 us
    all_to_all x1, starting transfers between devices, left_gradient(): lax.all_to_all(term.reshape(peers, block_size // peers, block_size), 'dp'...  39.7 us
    all_to_all x1, waiting for transfers between devices, left_gradient(): lax.all_to_all(term.reshape(peers, block_size // peers, block_size), 'dp'...  29.2 us
    pallas_call x1, Pallas kernels, build_maps(): pl.pallas_call(whole_kernel, grid=(count, count), in_specs=[pl.BlockSpec(...  26.8 us
    gather x1, local copies, waits for them, and re-layouts, build_maps(): rows = jnp.take(left_full, inverse, axis=0)  17.6 us
  transfers between devices with their start and end apart: 3, of which 3 were waited for; matrix products, arithmetic and copies ran while one was open for 6% of the time, Pallas kernels for 0%

profile of v5, /device:TPU:1, one launch (start us, length us, event | category | flops | bytes accessed | tf_op | source)
XLA Modules:
  0.0 637.7 jit_solution(15793311026085913930)
XLA Ops:
  7.2 0.0 all-gather.7.cloned.1.call-start
  7.2 0.7 all-gather.7.cloned.1.call-update
  7.9 0.0 all-gather.5.cloned.1.call-start
  7.9 0.7 all-gather.5.cloned.1.call-update
  8.6 0.7 compare_select_fusion
  9.4 11.8 %scatter_custom_fusion = s32[3072]{0:T(1024)S(1)} fusion(s32[3072]{0:T(1024)S(1)} %bitcast.36, s32[3072]{0:T(1024)S(1)} %iota.14, s32[]{:T(128)} %constant.18.clone.1), kind=kCustom, calls=%fused_computation.26 | custom fusion | bytes 12292 | tf_op jit(solution)/shard_map/scatter | solution.py:27
  21.2 1.7 copy.8.owner_ref
  22.9 2.4 copy.9.gain_ref
  25.3 0.7 slice_reduce_fusion
  26.0 56.3 %all-gather.7.cloned.1.call-done = bf16[1,3072,768]{2,1,0:T(8,128)(2,1)} async-done(((bf16[1,96,768]{2,1,0:T(8,128)(2,1)}), bf16[1,3072,768]{2,1,0:T(8,128)(2,1)}) %all-gather.7.cloned.1.call-update) | async-done | bytes 4718608 | tf_op jit(solution)/shard_map/all_gather | solution.py:230
  82.3 17.6 %gather_fusion = bf16[3072,768]{1,0:T(8,128)(2,1)} fusion(bf16[3072,768]{1,0:T(8,128)(2,1)} %bitcast.27, s32[3072]{0:T(1024)S(1)} %get-tuple-element.9), kind=kCustom, calls=%fused_computation | custom fusion | bytes 9449472 | tf_op jit(solution)/shard_map/jit(_take)/gather | solution.py:28
  99.9 5.7 broadcast_select_fusion.rows_ref
  105.6 44.2 %all-gather.5.cloned.1.call-done = bf16[1,3072,768]{2,1,0:T(8,128)(2,1)} async-done(((bf16[1,96,768]{2,1,0:T(8,128)(2,1)}), bf16[1,3072,768]{2,1,0:T(8,128)(2,1)}) %all-gather.5.cloned.1.call-update) | async-done | bytes 4718608 | tf_op jit(solution)/shard_map/all_gather | solution.py:231
  149.8 0.0 copy-start
  149.8 0.0 copy-start.1
  149.8 26.8 %whole_map.1.whole_ref = bf16[3072,3072]{1,0:T(8,128)(2,1)} custom-call(bf16[3072,768]{1,0:T(8,128)(2,1)} %bitcast.29, bf16[3072,768]{1,0:T(8,128)(2,1)} %broadcast_select_fusion.rows_ref, s32[3072,1]{1,0:T(8,128)} %copy.8.owner_ref, f32[3072,1]{1,0:T(8,128)} %copy.9.gain_ref), custom_call_target="tpu_custom_call" | custom-call | tf_op jit(solution)/shard_map/whole_map/pallas_call | solution.py:29
  176.6 0.0 copy-done
  176.6 0.0 copy-done.1
  176.6 0.0 copy-start.3
  176.6 0.0 copy-start.2
  176.6 372.0 %relay.1 = (bf16[9,16,3072]{2,1,0:T(8,128)(2,1)S(1)}, bf16[9,16,3072]{2,1,0:T(8,128)(2,1)S(1)}, bf16[9,16,768]{2,1,0:T(8,128)(2,1)S(1)}) custom-call(bf16[9,16,3072]{2,1,0:T(8,128)(2,1)S(1)} %bitcast.24, bf16[9,16,3072]{2,1,0:T(8,128)(2,1)S(1)} %bitcast.25, bf16[3072,3072]{1,0:T(8,128)(2,1)} %whole_map.1.whole_ref), custom_call_target="tpu_custom_call" | custom-call | tf_op jit(solution)/shard_map/relay/pallas_call | solution.py:203
  548.6 0.2 fusion.7
  548.9 0.0 copy-done.3
  548.9 0.3 fusion.9
  549.2 0.0 copy-done.2
  549.2 5.9 fusion.4
  555.1 5.2 convolution_convert_fusion
  560.3 39.7 %all-to-all-start = ((bf16[32,24,768]{2,1,0:T(8,128)(2,1)}), bf16[32,24,768]{2,1,0:T(8,128)(2,1)S(1)}, u32[]{:S(2)}, u32[]{:S(2)}) async-start(bf16[32,24,768]{2,1,0:T(8,128)(2,1)} %bitcast.15), calls=%async_computation | async-start | bytes 2359296 | tf_op jit(solution)/shard_map/all_to_all | solution.py:253
  600.0 29.2 %all-to-all-done = bf16[32,24,768]{2,1,0:T(8,128)(2,1)S(1)} async-done(((bf16[32,24,768]{2,1,0:T(8,128)(2,1)}), bf16[32,24,768]{2,1,0:T(8,128)(2,1)S(1)}, u32[]{:S(2)}, u32[]{:S(2)}) %all-to-all-start) | async-done | bytes 1179680 | tf_op jit(solution)/shard_map/all_to_all | solution.py:253
  629.2 0.8 convert_reduce_fusion
  630.0 0.9 copy.11
  (5 shorter events, 0.0 us)
Async XLA Ops:
  7.2 75.2 %all-gather.7.cloned.1.call-start = ((), (), s32[]{:S(2)}) async-start(), calls=%async_computation.2 | async-start | bytes 4866048 | tf_op jit(solution)/shard_map/all_gather | solution.py:230
  7.9 141.9 %all-gather.5.cloned.1.call-start = ((), (), s32[]{:S(2)}) async-start(), calls=%async_computation.1 | async-start | bytes 4866048 | tf_op jit(solution)/shard_map/all_gather | solution.py:231
  149.8 26.8 %copy-start = (bf16[6,24,3072]{2,1,0:T(8,128)(2,1)S(1)}, bf16[6,24,3072]{2,1,0:T(8,128)(2,1)}, u32[]{:S(2)}) copy-start(bf16[6,24,3072]{2,1,0:T(8,128)(2,1)} %param.6) | copy-start | bytes 2654212
  149.8 26.8 %copy-start.1 = (bf16[6,24,3072]{2,1,0:T(8,128)(2,1)S(1)}, bf16[6,24,3072]{2,1,0:T(8,128)(2,1)}, u32[]{:S(2)}) copy-start(bf16[6,24,3072]{2,1,0:T(8,128)(2,1)} %param.7) | copy-start | bytes 2654212
  176.6 372.3 %copy-start.3 = (f32[1,3072]{1,0:T(1,128)S(1)}, f32[1,3072]{1,0:T(1,128)}, u32[]{:S(2)}) copy-start(f32[1,3072]{1,0:T(1,128)} %param.8) | copy-start | bytes 36868
  176.6 372.6 %copy-start.2 = (bf16[1,3072,768]{2,1,0:T(8,128)(2,1)S(1)}, bf16[1,3072,768]{2,1,0:T(8,128)(2,1)}, u32[]{:S(2)}) copy-start(bf16[1,3072,768]{2,1,0:T(8,128)(2,1)} %all-gather.5.cloned.1.call-done) | copy-start | bytes 14155780
  560.3 68.9 %all-to-all-start = ((bf16[32,24,768]{2,1,0:T(8,128)(2,1)}), bf16[32,24,768]{2,1,0:T(8,128)(2,1)S(1)}, u32[]{:S(2)}, u32[]{:S(2)}) async-start(bf16[32,24,768]{2,1,0:T(8,128)(2,1)} %bitcast.15), calls=%async_computation | async-start | bytes 2359296 | tf_op jit(solution)/shard_map/all_to_all | solution.py:253
Sparse Core Ops, SparseCore 0:
  10.1 72.1 all-gather.6
  84.5 65.2 all-gather.4
